TPU v7x, 32 devices: a whole 2x2x4 slice. The times are simulated.
32 devices in a mesh: dp: 8 (over z, y), tensor: 4 (over x, core).
Axes of the slice: x: 2, y: 2, z: 4, core: 2. Of those that a mesh axis runs over, the one named last changes fastest.
Arguments:
- inputs: bfloat16 [8192, 512], P(('dp', 'tensor')), may hold values from -13 to 13
- lengths: int32 [8], P('dp'), may hold values from 256 to 1024, as said below
- cotangent: bfloat16 [8192, 512], P(('dp', 'tensor')), may hold values from -6 to 6
- query_weight: bfloat16 [512, 512], P('dp', 'tensor'), may hold values from -0.25 to 0.25
- key_weight: bfloat16 [512, 512], P('dp', 'tensor'), may hold values from -0.25 to 0.25
- value_weight: bfloat16 [512, 512], P('dp', 'tensor'), may hold values from -0.25 to 0.25
- output_weight: bfloat16 [512, 512], P('tensor', 'dp'), may hold values from -1 to 1
- inner_weight: bfloat16 [512, 2048], P('dp', 'tensor'), may hold values from -0.25 to 0.25
- outer_weight: bfloat16 [2048, 512], P('tensor', 'dp'), may hold values from -0.125 to 0.125
- first_gain: bfloat16 [512], P('dp'), may hold values from 0.099609375 to 1.8984375
- second_gain: bfloat16 [512], P('dp'), may hold values from 0.099609375 to 1.8984375
Outputs:
- outputs: bfloat16 [8192, 512], P(('dp', 'tensor'))
- input_grad: bfloat16 [8192, 512], P(('dp', 'tensor'))
- query_weight_grad: float32 [512, 512], P('dp', 'tensor')
- key_weight_grad: float32 [512, 512], P('dp', 'tensor')
- value_weight_grad: float32 [512, 512], P('dp', 'tensor')
- output_weight_grad: float32 [512, 512], P('tensor', 'dp')
- inner_weight_grad: float32 [512, 2048], P('dp', 'tensor')
- outer_weight_grad: float32 [2048, 512], P('tensor', 'dp')
- first_gain_grad: float32 [512], P('dp')
- second_gain_grad: float32 [512], P('dp')
- root_mean_squares: float32 [3], replicated
Inputs may be any that keep to these rules, and one draw needn't show every extreme that they name: `lengths`: one sequence of every draw is whole.
All inputs are finite; a program needn't handle non-finite values.
Results may differ from a plain program's by a relative error of at most 0.017.
Values may be sent and summed in bfloat16 or wider, within the bound.
A program may use at most 320 MiB of HBM per device.

v0:
```python
import jax
import jax.numpy as jnp
from jax import lax
from jax.sharding import PartitionSpec as P

HEAD_DIM = 64
BLOCK = 16


top_level = lax.Precision.HIGHEST


def cut_along(x, dim, peers):
    before, after = (x.shape[:dim], x.shape[dim + 1 :])
    return jnp.moveaxis(x.reshape(*before, peers, -1, *after), dim, 0)


def sent_and_summed(x, axis, dim):
    parts = cut_along(x, dim, lax.axis_size(axis))
    arrived = lax.all_to_all(parts, axis, split_axis=0, concat_axis=0, tiled=True)
    return arrived.astype(jnp.float32).sum(axis=0)


def sent_together(arrays, axis, dim, along):
    ends, at = ([], 0)
    for a in arrays[:-1]:
        at += a.shape[along]
        ends.append(at)
    both = jnp.concatenate(arrays, axis=along)
    return tuple(jnp.split(sent_and_summed(both, axis, dim), ends, axis=along))


def neighbours(blocks):
    padded = jnp.pad(blocks, ((1, 1),) + ((0, 0),) * (blocks.ndim - 1))
    return jnp.concatenate([padded[:-2], padded[1:-1], padded[2:]], axis=1)


def level_terms(queries, key_rows, value_rows, valid_rows, factor):
    sequence_len, width_per_head = queries.shape
    pooled_level = sequence_len // factor
    coarse_q = jnp.mean(queries.reshape(pooled_level, factor, width_per_head), axis=1)
    counts = jnp.sum(valid_rows.reshape(pooled_level, factor), axis=1)
    divisor = jnp.maximum(counts, 1.0)[:, None]
    coarse_k = (
        jnp.sum(
            (key_rows * valid_rows[:, None]).reshape(pooled_level, factor, width_per_head), axis=1
        )
        / divisor
    )
    coarse_v = (
        jnp.sum(
            (value_rows * valid_rows[:, None]).reshape(pooled_level, factor, width_per_head), axis=1
        )
        / divisor
    )
    blocks = pooled_level // BLOCK
    query_block_rows = coarse_q.reshape(blocks, BLOCK, width_per_head)
    nearby_key_rows = neighbours(coarse_k.reshape(blocks, BLOCK, width_per_head))
    nearby_value_rows = neighbours(coarse_v.reshape(blocks, BLOCK, width_per_head))
    c_near = neighbours(counts.reshape(blocks, BLOCK))
    if factor > 1:
        logit_scores = jnp.einsum(
            "une,uhe->unh", query_block_rows, nearby_key_rows, precision=top_level
        ) * width_per_head ** (-0.5)
    else:
        logit_scores = jnp.einsum(
            "une,uhe->unh", query_block_rows, nearby_key_rows, preferred_element_type=jnp.float32
        ) * width_per_head ** (-0.5)
    weights = jnp.broadcast_to(c_near[:, None, :], logit_scores.shape)
    if factor > 1:
        block_ids = jnp.arange(blocks, dtype=jnp.int32)[:, None]
        q_pos = block_ids * BLOCK + jnp.arange(BLOCK, dtype=jnp.int32)[None, :]
        k_pos = (block_ids - 1) * BLOCK + jnp.arange(3 * BLOCK, dtype=jnp.int32)[None, :]
        half_block = BLOCK // 2
        apart = jnp.abs(q_pos[:, :, None] // half_block - k_pos[:, None, :] // half_block) > 1
        weights = jnp.where(apart, weights, 0.0)
    is_live = weights > 0.0
    row_top = jnp.max(jnp.where(is_live, logit_scores, -1e30), axis=-1)
    safe_top = jnp.where(row_top > -1e29, row_top, 0.0)
    weighted_values = weights * jnp.exp(logit_scores - safe_top[..., None])
    softmax_numerator = jnp.einsum(
        "vwg,vgi->vwi", weighted_values, nearby_value_rows, precision=top_level
    ).reshape(pooled_level, width_per_head)
    denominator = jnp.sum(weighted_values, axis=-1).reshape(pooled_level)
    row_top = row_top.reshape(pooled_level)
    return (
        jnp.repeat(softmax_numerator, factor, axis=0),
        jnp.repeat(denominator, factor),
        jnp.repeat(row_top, factor),
    )


def hierarchy(queries, key_rows, value_rows, valid_len):
    sequence_len = queries.shape[0]
    valid_rows = (jnp.arange(sequence_len, dtype=jnp.int32) < valid_len).astype(jnp.float32)
    depth = (sequence_len // BLOCK).bit_length() - 1
    levels_out = [
        level_terms(queries, key_rows, value_rows, valid_rows, 2**level) for level in range(depth)
    ]
    overall = levels_out[0][2]
    for entry in levels_out[1:]:
        overall = jnp.maximum(overall, entry[2])
    softmax_numerator = levels_out[0][0] * jnp.exp(levels_out[0][2] - overall)[:, None]
    denominator = levels_out[0][1] * jnp.exp(levels_out[0][2] - overall)
    for entry in levels_out[1:]:
        factor_now = jnp.exp(entry[2] - overall)
        softmax_numerator = softmax_numerator + entry[0] * factor_now[:, None]
        denominator = denominator + entry[1] * factor_now
    return softmax_numerator / denominator[:, None]


def layer_norm(residual, gain_values):
    row_mean = jnp.mean(residual, axis=-1, keepdims=True)
    centred = residual - row_mean
    variance = jnp.mean(centred * centred, axis=-1, keepdims=True)
    return centred * lax.rsqrt(variance + 1e-05) * gain_values


def gelu_tanh(values):
    return jax.nn.gelu(values, approximate=True)


def per_device(
    inputs,
    lengths,
    cotangent,
    query_weight,
    key_weight,
    value_weight,
    output_weight,
    inner_weight,
    outer_weight,
    first_gain,
    second_gain,
):
    rows_dev = inputs.shape[0]
    tensors = lax.axis_size("tensor")
    sequences = lengths.shape[0]
    group_rows = rows_dev * tensors
    sequence_len = group_rows // sequences
    query_full, key_full, value_full, output_full, inner_full, outer_full, gain_one, gain_two = (
        lax.all_gather(query_weight, "dp", axis=0, tiled=True),
        lax.all_gather(key_weight, "dp", axis=0, tiled=True),
        lax.all_gather(value_weight, "dp", axis=0, tiled=True),
        lax.all_gather(output_weight, "dp", axis=1, tiled=True),
        lax.all_gather(inner_weight, "dp", axis=0, tiled=True),
        lax.all_gather(outer_weight, "dp", axis=1, tiled=True),
        lax.all_gather(first_gain, "dp", axis=0, tiled=True),
        lax.all_gather(second_gain, "dp", axis=0, tiled=True),
    )
    inner_dim = query_full.shape[1]
    heads_here = inner_dim // HEAD_DIM
    residual = inputs.astype(jnp.float32)
    normed_one, norm_one_back = jax.vjp(layer_norm, residual, gain_one.astype(jnp.float32))
    normed_one_low = normed_one.astype(jnp.bfloat16)
    normed_all = lax.all_gather(normed_one_low, "tensor", axis=0, tiled=True)
    joint_weight = jnp.concatenate([query_full, key_full, value_full], axis=1)
    projected = jnp.dot(normed_all, joint_weight, preferred_element_type=jnp.float32).astype(
        jnp.bfloat16
    )

    def split_heads(matrix):
        return (
            matrix.astype(jnp.float32)
            .reshape(sequences, sequence_len, heads_here, HEAD_DIM)
            .transpose(0, 2, 1, 3)
            .reshape(sequences * heads_here, sequence_len, HEAD_DIM)
        )

    def merge_heads(stacked):
        return (
            stacked.reshape(sequences, heads_here, sequence_len, HEAD_DIM)
            .transpose(0, 2, 1, 3)
            .reshape(group_rows, inner_dim)
        )

    head_lens = jnp.repeat(lengths, heads_here)

    def attend(queries, key_rows, value_rows):
        return jax.vmap(hierarchy)(queries, key_rows, value_rows, head_lens)

    attended, attend_back = jax.vjp(
        attend,
        split_heads(projected[:, :inner_dim]),
        split_heads(projected[:, inner_dim : 2 * inner_dim]),
        split_heads(projected[:, 2 * inner_dim :]),
    )
    attended_group = merge_heads(attended).astype(jnp.bfloat16)
    attention_branch = lax.psum_scatter(
        jnp.dot(attended_group, output_full, preferred_element_type=jnp.float32).astype(
            jnp.bfloat16
        ),
        "tensor",
        scatter_dimension=0,
        tiled=True,
    ).astype(jnp.float32)
    middle = residual + attention_branch
    normed_two, norm_two_back = jax.vjp(layer_norm, middle, gain_two.astype(jnp.float32))
    normed_low = normed_two.astype(jnp.bfloat16)
    second_all = lax.all_gather(normed_low, "tensor", axis=0, tiled=True)
    pre_act = jnp.dot(second_all, inner_full, preferred_element_type=jnp.float32)
    activated, gelu_back = jax.vjp(gelu_tanh, pre_act)
    activated_low = activated.astype(jnp.bfloat16)
    dense_branch = lax.psum_scatter(
        jnp.dot(activated_low, outer_full, preferred_element_type=jnp.float32).astype(jnp.bfloat16),
        "tensor",
        scatter_dimension=0,
        tiled=True,
    ).astype(jnp.float32)
    result = middle + dense_branch
    row_ids = lax.axis_index("tensor") * rows_dev + jnp.arange(rows_dev, dtype=jnp.int32)
    seq_ids = row_ids // sequence_len
    positions = row_ids % sequence_len
    row_limits = jnp.sum(
        jnp.where(
            seq_ids[:, None] == jnp.arange(sequences, dtype=jnp.int32)[None, :], lengths[None, :], 0
        ),
        axis=1,
    )
    valid_rows = (positions < row_limits).astype(jnp.float32)
    result_sq = jnp.sum(valid_rows * jnp.sum(result * result, axis=1))
    first_sq = jnp.sum(valid_rows * jnp.sum(attention_branch * attention_branch, axis=1))
    second_sq = jnp.sum(valid_rows * jnp.sum(dense_branch * dense_branch, axis=1))
    valid_count = jnp.sum(valid_rows)
    stat_totals = lax.psum((result_sq, first_sq, second_sq, valid_count), ("dp", "tensor"))
    cot_all = lax.all_gather(cotangent, "tensor", axis=0, tiled=True)
    act_grad = jnp.dot(cot_all, outer_full.T, preferred_element_type=jnp.float32)
    (pre_grad,) = gelu_back(act_grad)
    pre_low = pre_grad.astype(jnp.bfloat16)
    inner_grad = jnp.dot(second_all.T, pre_low, preferred_element_type=jnp.float32)
    outer_grad = jnp.dot(activated_low.T, cot_all, preferred_element_type=jnp.float32)
    normed_grad = lax.psum_scatter(
        jnp.dot(pre_low, inner_full.T, preferred_element_type=jnp.float32).astype(jnp.bfloat16),
        "tensor",
        scatter_dimension=0,
        tiled=True,
    ).astype(jnp.float32)
    middle_part, gain_two_grad = norm_two_back(normed_grad)
    middle_grad = cotangent.astype(jnp.float32) + middle_part
    branch_low = middle_grad.astype(jnp.bfloat16)
    branch_all = lax.all_gather(branch_low, "tensor", axis=0, tiled=True)
    attended_grad = jnp.dot(branch_all, output_full.T, preferred_element_type=jnp.float32)
    output_grad = jnp.dot(attended_group.T, branch_all, preferred_element_type=jnp.float32)
    query_grad, key_rows_grad, value_rows_grad = attend_back(split_heads(attended_grad))
    joint_low = jnp.concatenate(
        [merge_heads(query_grad), merge_heads(key_rows_grad), merge_heads(value_rows_grad)], axis=1
    ).astype(jnp.bfloat16)
    joint_grad = jnp.dot(normed_all.T, joint_low, preferred_element_type=jnp.float32)
    query_grad_t = joint_grad[:, :inner_dim]
    key_grad_t = joint_grad[:, inner_dim : 2 * inner_dim]
    value_grad_t = joint_grad[:, 2 * inner_dim :]
    normed_one_grad = lax.psum_scatter(
        jnp.dot(joint_low, joint_weight.T, preferred_element_type=jnp.float32).astype(jnp.bfloat16),
        "tensor",
        scatter_dimension=0,
        tiled=True,
    ).astype(jnp.float32)
    input_part, gain_one_grad = norm_one_back(normed_one_grad)
    input_grad = (middle_grad + input_part).astype(jnp.bfloat16)
    shard_grads = (
        *sent_together(
            (
                query_grad_t.astype(jnp.bfloat16),
                key_grad_t.astype(jnp.bfloat16),
                value_grad_t.astype(jnp.bfloat16),
            ),
            "dp",
            0,
            1,
        ),
        sent_and_summed(output_grad.astype(jnp.bfloat16), "dp", 1),
        sent_and_summed(inner_grad.astype(jnp.bfloat16), "dp", 0),
        sent_and_summed(outer_grad.astype(jnp.bfloat16), "dp", 1),
    )
    gain_totals = lax.psum((gain_one_grad, gain_two_grad), ("dp", "tensor"))
    piece_len = first_gain.shape[0]
    offset = lax.axis_index("dp") * piece_len
    first_slice = lax.dynamic_slice_in_dim(gain_totals[0], offset, piece_len)
    second_slice = lax.dynamic_slice_in_dim(gain_totals[1], offset, piece_len)
    squares_all = jnp.stack([stat_totals[0], stat_totals[1], stat_totals[2]])
    root_mean_squares = jnp.sqrt(squares_all / (stat_totals[3] * inputs.shape[1]))
    return (
        result.astype(jnp.bfloat16),
        input_grad,
        shard_grads[0],
        shard_grads[1],
        shard_grads[2],
        shard_grads[3],
        shard_grads[4],
        shard_grads[5],
        first_slice,
        second_slice,
        root_mean_squares,
    )


def solution(mesh):
    return jax.shard_map(
        per_device,
        mesh=mesh,
        in_specs=(
            P(("dp", "tensor"), None),
            P("dp"),
            P(("dp", "tensor"), None),
            P("dp", "tensor"),
            P("dp", "tensor"),
            P("dp", "tensor"),
            P("tensor", "dp"),
            P("dp", "tensor"),
            P("tensor", "dp"),
            P("dp"),
            P("dp"),
        ),
        out_specs=(
            P(("dp", "tensor"), None),
            P(("dp", "tensor"), None),
            P("dp", "tensor"),
            P("dp", "tensor"),
            P("dp", "tensor"),
            P("tensor", "dp"),
            P("dp", "tensor"),
            P("tensor", "dp"),
            P("dp"),
            P("dp"),
            P(),
        ),
        check_vma=False,
    )
```

profile of v0, /device:TPU:0, one launch (start us, length us, event | category | flops | bytes accessed | tf_op | source)
XLA Modules:
  0.0 768.6 jit_solution(11924971117627966690)
XLA Ops:
  13.2 23.7 %all-reduce.57 = (bf16[512]{0:T(512)(128)(2,1)S(1)}, bf16[512]{0:T(512)(128)(2,1)}) all-reduce(bf16[512]{0:T(512)(128)(2,1)S(1)} %dynamic-update-slice, bf16[512]{0:T(512)(128)(2,1)S(1)} %dynamic-update-slice.1), channel_id=1, replica_groups=mesh['dp'=8,'tensor'=4] {'dp'}, use_global_device_ids=true, to_apply=%add.54 | all-reduce | flops 1024 | bytes 4096
  44.1 32.2 %all_gather.41 = bf16[128,512]{0,1:T(8,128)(2,1)} all-gather(bf16[128,64]{0,1:T(8,128)(2,1)} %param.17), channel_id=1, replica_groups=mesh['dp'=8,'tensor'=4] {'dp'}, dimensions={1}, use_global_device_ids=true | all-gather | bytes 147456 | tf_op jit(solution)/shard_map/all_gather | solution.py:145
  76.3 30.6 %all_gather.38 = bf16[512,128]{1,0:T(8,128)(2,1)S(1)} all-gather(bf16[64,128]{1,0:T(8,128)(2,1)S(1)} %copy-done.364), channel_id=1, replica_groups=mesh['dp'=8,'tensor'=4] {'dp'}, dimensions={0}, use_global_device_ids=true | all-gather | bytes 147456 | tf_op jit(solution)/shard_map/all_gather | solution.py:142
  106.9 30.5 %all_gather.39 = bf16[512,128]{1,0:T(8,128)(2,1)S(1)} all-gather(bf16[64,128]{1,0:T(8,128)(2,1)S(1)} %copy-done.365), channel_id=1, replica_groups=mesh['dp'=8,'tensor'=4] {'dp'}, dimensions={0}, use_global_device_ids=true | all-gather | bytes 147456 | tf_op jit(solution)/shard_map/all_gather | solution.py:143
  137.4 30.8 %all_gather.40 = bf16[512,128]{1,0:T(8,128)(2,1)S(1)} all-gather(bf16[64,128]{1,0:T(8,128)(2,1)S(1)} %copy-done.366), channel_id=1, replica_groups=mesh['dp'=8,'tensor'=4] {'dp'}, dimensions={0}, use_global_device_ids=true | all-gather | bytes 147456 | tf_op jit(solution)/shard_map/all_gather | solution.py:144
  203.1 3.5 select_reduce_fusion
  211.8 6.5 multiply_reduce_fusion.7
  251.8 3.5 convert_reduce_fusion.2
  282.2 20.2 %reduce-scatter.5.cloned.1.call-done = bf16[256,512]{1,0:T(8,128)(2,1)} async-done(((bf16[1024,512]{1,0:T(8,128)(2,1)}), bf16[256,512]{1,0:T(8,128)(2,1)}) %reduce-scatter.5.cloned.1.call-update) | async-done | bytes 262160 | tf_op jit(solution)/shard_map/reduce_scatter | solution.py:189
  307.6 33.6 %all_gather.44 = bf16[512,512]{1,0:T(8,128)(2,1)} all-gather(bf16[64,512]{1,0:T(8,128)(2,1)} %param.18), channel_id=1, replica_groups=mesh['dp'=8,'tensor'=4] {'dp'}, dimensions={0}, use_global_device_ids=true | all-gather | bytes 589824 | tf_op jit(solution)/shard_map/all_gather | solution.py:146
  341.2 34.0 %all_gather.45 = bf16[512,512]{0,1:T(8,128)(2,1)} all-gather(bf16[512,64]{0,1:T(8,128)(2,1)} %param.19), channel_id=1, replica_groups=mesh['dp'=8,'tensor'=4] {'dp'}, dimensions={1}, use_global_device_ids=true | all-gather | bytes 589824 | tf_op jit(solution)/shard_map/all_gather | solution.py:147
  375.1 3.4 fusion.407
  378.5 5.2 fusion.10
  386.5 3.5 convolution_convert_fusion.3
  393.0 18.5 %reduce-scatter.9.cloned.1.call-done = bf16[256,512]{1,0:T(8,128)(2,1)} async-done(((bf16[1024,512]{1,0:T(8,128)(2,1)}), bf16[256,512]{1,0:T(8,128)(2,1)}) %reduce-scatter.9.cloned.1.call-update) | async-done | bytes 262160 | tf_op jit(solution)/shard_map/reduce_scatter | solution.py:232
  411.5 27.2 %reduce-scatter.7.cloned.1.call-done = bf16[256,512]{1,0:T(8,128)(2,1)} async-done(((bf16[1024,512]{1,0:T(8,128)(2,1)}), bf16[256,512]{1,0:T(8,128)(2,1)}) %reduce-scatter.7.cloned.1.call-update) | async-done | bytes 262160 | tf_op jit(solution)/shard_map/reduce_scatter | solution.py:204
  489.3 3.7 convolution_convert_fusion.5
  493.1 5.8 all-to-all-start.3
  505.9 4.1 fusion.33
  511.4 5.4 fusion.60
  583.8 3.7 multiply_reduce_fusion.1
  604.5 5.4 add_reduce_fusion
  611.3 7.2 multiply_reduce_fusion
  629.2 5.5 fusion.401
  639.1 7.6 fusion.65
  669.3 6.0 all-to-all-start.2
  678.3 10.8 %all-to-all-done.2 = bf16[8,64,512]{2,1,0:T(8,128)(2,1)S(1)} async-done(((bf16[8,64,512]{2,1,0:T(8,128)(2,1)}), bf16[8,64,512]{2,1,0:T(8,128)(2,1)S(1)}, u32[]{:S(2)}, u32[]{:S(2)}) %all-to-all-start.2) | async-done | bytes 524320 | tf_op jit(solution)/shard_map/all_to_all | solution.py:20
  689.0 3.6 all-to-all-start.1
  695.5 4.5 all-to-all-done.1
  700.0 3.5 all-to-all-start
  707.3 5.9 all-to-all-done
  716.4 38.9 %all-reduce.56 = (f32[512]{0:T(512)S(1)}, f32[512]{0:T(512)S(1)}, f32[1]{0:T(128)}, f32[1]{0:T(128)}, f32[1]{0:T(128)}, /*index=5*/f32[]{:T(128)}) all-reduce(f32[512]{0:T(512)S(1)} %get-tuple-element.24, f32[512]{0:T(512)S(1)} %copy-done.379, f32[1]{0:T(128)} %bitcast.119, ...), channel_id=1, replica_groups=mesh['dp'=8,'tensor'=4] {'dp','tensor'}, use_global_device_ids=true, to_apply=%region_83.84 | all-reduce | flops 1028 | bytes 8224 | tf_op jit(solution)/shard_map/psum | solution.py:275
  (1263 shorter events, 318.3 us)
Async XLA Ops:
  7.2 69.1 %copy-start.364 = (bf16[64,128]{1,0:T(8,128)(2,1)S(1)}, bf16[64,128]{1,0:T(8,128)(2,1)}, u32[]{:S(2)}) copy-start(bf16[64,128]{1,0:T(8,128)(2,1)} %param.14) | copy-start | bytes 49156
  7.2 99.7 %copy-start.365 = (bf16[64,128]{1,0:T(8,128)(2,1)S(1)}, bf16[64,128]{1,0:T(8,128)(2,1)}, u32[]{:S(2)}) copy-start(bf16[64,128]{1,0:T(8,128)(2,1)} %param.15) | copy-start | bytes 49156
  7.2 130.2 %copy-start.366 = (bf16[64,128]{1,0:T(8,128)(2,1)S(1)}, bf16[64,128]{1,0:T(8,128)(2,1)}, u32[]{:S(2)}) copy-start(bf16[64,128]{1,0:T(8,128)(2,1)} %param.16) | copy-start | bytes 49156
  7.2 167.4 %all-gather.5.cloned.1.call-start = ((), (), s32[]{:S(2)}) async-start(), calls=%async_computation.8 | async-start | bytes 1310720 | tf_op jit(solution)/shard_map/all_gather | solution.py:156
  8.3 32.3 %copy-start.294 = (f32[256]{0:T(256)}, f32[256]{0:T(256)S(1)}, u32[]{:S(2)}) copy-start(f32[256]{0:T(256)S(1)} %broadcast_multiply_fusion.6) | copy-start | bytes 3076
  9.5 31.1 %copy-start.372 = (f32[256]{0:T(256)}, f32[256]{0:T(256)S(1)}, u32[]{:S(2)}) copy-start(f32[256]{0:T(256)S(1)} %fusion.317) | copy-start | bytes 3076
  36.9 131.3 %copy-start.286 = (f32[512]{0:T(512)}, f32[512]{0:T(512)S(1)}, u32[]{:S(2)}) copy-start(f32[512]{0:T(512)S(1)} %convert_element_type.195) | copy-start | bytes 6148
  38.8 263.6 %reduce-scatter.5.cloned.1.call-start = ((), (), s32[]{:S(2)}) async-start(), calls=%async_computation.9 | async-start | bytes 1310720 | tf_op jit(solution)/shard_map/reduce_scatter | solution.py:189
  40.7 127.5 %copy-start.356 = (f32[512]{0:T(512)}, f32[512]{0:T(512)S(1)}, u32[]{:S(2)}) copy-start(f32[512]{0:T(512)S(1)} %fusion.185) | copy-start | bytes 6148
  43.4 124.9 %copy-start.387 = (f32[64]{0:T(128)}, f32[64]{0:T(128)S(1)}, u32[]{:S(2)}) copy-start(f32[64]{0:T(128)S(1)} %get-tuple-element.233) | copy-start | bytes 772
  171.2 91.6 %copy-start.166 = (f32[2,16,48]{2,1,0:T(8,128)}, f32[2,16,48]{2,1,0:T(8,128)S(1)}, u32[]{:S(2)}) copy-start(f32[2,16,48]{2,1,0:T(8,128)S(1)} %pad_maximum_fusion.49) | copy-start | bytes 18436
  172.0 47.8 %copy-start.101 = (f32[2,32,48]{2,1,0:T(8,128)}, f32[2,32,48]{2,1,0:T(8,128)S(1)}, u32[]{:S(2)}) copy-start(f32[2,32,48]{2,1,0:T(8,128)S(1)} %pad_maximum_fusion.48) | copy-start | bytes 36868
  173.7 50.2 %copy-start.177 = (pred[8,16,48]{2,1,0:T(8,128)(4,1)}, pred[8,16,48]{2,1,0:T(8,128)(4,1)S(1)}, u32[]{:S(2)}) copy-start(pred[8,16,48]{2,1,0:T(8,128)(4,1)S(1)} %abs_compare_fusion.2) | copy-start | bytes 18436
  174.4 65.2 %copy-start.114 = (pred[16,16,48]{2,1,0:T(8,128)(4,1)}, pred[16,16,48]{2,1,0:T(8,128)(4,1)S(1)}, u32[]{:S(2)}) copy-start(pred[16,16,48]{2,1,0:T(8,128)(4,1)S(1)} %abs_compare_fusion.1) | copy-start | bytes 36868
  174.6 45.3 %copy-start.67 = (pred[32,16,48]{2,1,0:T(8,128)(4,1)}, pred[32,16,48]{2,1,0:T(8,128)(4,1)S(1)}, u32[]{:S(2)}) copy-start(pred[32,16,48]{2,1,0:T(8,128)(4,1)S(1)} %abs_compare_fusion) | copy-start | bytes 73732
  195.4 44.2 %copy-start.170 = (f32[2,16,16]{2,1,0:T(8,128)}, f32[2,16,16]{2,1,0:T(8,128)S(1)}, u32[]{:S(2)}) copy-start(f32[2,16,16]{2,1,0:T(8,128)S(1)} %get-tuple-element.213) | copy-start | bytes 6148
  196.1 43.5 %copy-start.203 = (f32[2,16,16]{2,1,0:T(8,128)}, f32[2,16,16]{2,1,0:T(8,128)S(1)}, u32[]{:S(2)}) copy-start(f32[2,16,16]{2,1,0:T(8,128)S(1)} %compare_select_fusion.5) | copy-start | bytes 6148
  199.2 44.6 %copy-start.184 = (f32[2,4,16,64]{3,2,1,0:T(8,128)}, f32[2,4,16,64]{3,2,1,0:T(8,128)S(1)}, u32[]{:S(2)}) copy-start(f32[2,4,16,64]{3,2,1,0:T(8,128)S(1)} %get-tuple-element.193) | copy-start | bytes 98308
  222.6 36.0 %copy-start.28 = (f32[2,32,16,48]{3,2,1,0:T(8,128)}, f32[2,32,16,48]{3,2,1,0:T(8,128)S(1)}, u32[]{:S(2)}) copy-start(f32[2,32,16,48]{3,2,1,0:T(8,128)S(1)} %get-tuple-element.216) | copy-start | bytes 589828
  280.2 95.0 %all-gather.9.cloned.1.call-start = ((), (), s32[]{:S(2)}) async-start(), calls=%async_computation.12 | async-start | bytes 1310720 | tf_op jit(solution)/shard_map/all_gather | solution.py:226
  280.9 97.6 %all-gather.7.cloned.1.call-start = ((), (), s32[]{:S(2)}) async-start(), calls=%async_computation.10 | async-start | bytes 1310720 | tf_op jit(solution)/shard_map/all_gather | solution.py:200
  307.5 104.0 %reduce-scatter.9.cloned.1.call-start = ((), (), s32[]{:S(2)}) async-start(), calls=%async_computation.13 | async-start | bytes 1310720 | tf_op jit(solution)/shard_map/reduce_scatter | solution.py:232
  386.4 52.3 %reduce-scatter.7.cloned.1.call-start = ((), (), s32[]{:S(2)}) async-start(), calls=%async_computation.11 | async-start | bytes 1310720 | tf_op jit(solution)/shard_map/reduce_scatter | solution.py:204
  390.0 112.0 %all-gather.11.cloned.1.call-start = ((), (), s32[]{:S(2)}) async-start(), calls=%async_computation.14 | async-start | bytes 1310720 | tf_op jit(solution)/shard_map/all_gather | solution.py:241
  493.1 176.2 %all-to-all-start.3 = ((bf16[8,512,64]{1,2,0:T(8,128)(2,1)}), bf16[8,512,64]{1,2,0:T(8,128)(2,1)}, u32[]{:S(2)}, u32[]{:S(2)}) async-start(bf16[8,512,64]{1,2,0:T(8,128)(2,1)} %bitcast.116), calls=%async_computation.7 | async-start | bytes 1048576 | tf_op jit(solution)/shard_map/all_to_all | solution.py:20
  669.3 19.8 %all-to-all-start.2 = ((bf16[8,64,512]{2,1,0:T(8,128)(2,1)}), bf16[8,64,512]{2,1,0:T(8,128)(2,1)S(1)}, u32[]{:S(2)}, u32[]{:S(2)}) async-start(bf16[8,64,512]{2,1,0:T(8,128)(2,1)} %bitcast.114), calls=%async_computation.6 | async-start | bytes 1048576 | tf_op jit(solution)/shard_map/all_to_all | solution.py:20
  675.3 38.6 %reduce-scatter.11.cloned.1.call-start = ((), (), s32[]{:S(2)}) async-start(), calls=%async_computation.15 | async-start | bytes 1310720 | tf_op jit(solution)/shard_map/reduce_scatter | solution.py:252
  689.0 11.0 %all-to-all-start.1 = ((bf16[8,128,64]{1,2,0:T(8,128)(2,1)}), bf16[8,128,64]{1,2,0:T(8,128)(2,1)S(1)}, u32[]{:S(2)}, u32[]{:S(2)}) async-start(bf16[8,128,64]{1,2,0:T(8,128)(2,1)} %bitcast.113), calls=%async_computation.5 | async-start | bytes 262144 | tf_op jit(solution)/shard_map/all_to_all | solution.py:20
  695.5 64.1 %copy-start.16 = (f32[256,512]{1,0:T(8,128)S(1)}, f32[256,512]{1,0:T(8,128)}, u32[]{:S(2)}) copy-start(f32[256,512]{1,0:T(8,128)} %copy-done.15) | copy-start | bytes 1572868
  695.5 64.1 %copy-start.23 = (bf16[256,512]{1,0:T(8,128)(2,1)S(1)}, bf16[256,512]{1,0:T(8,128)(2,1)}, u32[]{:S(2)}) copy-start(bf16[256,512]{1,0:T(8,128)(2,1)} %param.13) | copy-start | bytes 786436
  695.5 64.1 %copy-start.378 = (f32[256]{0:T(256)S(1)}, f32[256]{0:T(256)}, u32[]{:S(2)}) copy-start(f32[256]{0:T(256)} %copy-done.377) | copy-start | bytes 3076
  700.0 13.2 %all-to-all-start = ((bf16[8,64,384]{2,1,0:T(8,128)(2,1)}), bf16[8,64,384]{2,1,0:T(8,128)(2,1)S(1)}, u32[]{:S(2)}, u32[]{:S(2)}) async-start(bf16[8,64,384]{2,1,0:T(8,128)(2,1)} %bitcast.111), calls=%async_computation.4 | async-start | bytes 786432 | tf_op jit(solution)/shard_map/all_to_all | solution.py:20
  (374 other events, 2068.1 us)
Sparse Core Ops, SparseCore 0:
  38.9 14.0 all-gather.4
  280.3 22.0 reduce-scatter.4
  303.9 16.7 all-gather.8
  322.6 16.6 all-gather.6
  386.6 24.8 reduce-scatter.8
  413.9 24.7 reduce-scatter.6
  445.2 16.6 all-gather.10
  678.6 25.2 reduce-scatter.10
where the time goes:
time: 775 us; the launch traced here: 769 us
  blocking collectives  254 us (33%)
  local copies, waits for them, and re-layouts  148 us (19%)
  other arithmetic  130 us (17%)
  matrix products  107 us (14%)
  waiting for transfers between devices  87.9 us (11%)
  between operations  21.9 us (3%)
  starting transfers between devices  19.2 us (2%)
    dot_general x18, matrix products, level_terms(): jnp.einsum('vwg,vgi->vwi', weighted_values, nearby_value_rows, precision=...  39.5 us
    psum x1, blocking collectives, per_device(): gain_totals = lax.psum((gain_one_grad, gain_two_grad), ('dp', 'tensor'))  38.9 us
    all_gather x1, blocking collectives, per_device(): lax.all_gather(outer_weight, 'dp', axis=1, tiled=True)  34 us
    all_gather x1, blocking collectives, per_device(): lax.all_gather(inner_weight, 'dp', axis=0, tiled=True)  33.6 us
    all_gather x1, blocking collectives, per_device(): lax.all_gather(output_weight, 'dp', axis=1, tiled=True)  32.2 us
    all_gather x1, blocking collectives, per_device(): lax.all_gather(value_weight, 'dp', axis=0, tiled=True)  30.8 us
    all_gather x1, blocking collectives, per_device(): lax.all_gather(query_weight, 'dp', axis=0, tiled=True)  30.6 us
    all_gather x1, blocking collectives, per_device(): lax.all_gather(key_weight, 'dp', axis=0, tiled=True)  30.5 us
  transfers between devices with their start and end apart: 12, of which 6 were waited for; matrix products, arithmetic and copies ran while one was open for 32% of the time, Pallas kernels for 0%

commit v1 on v0

v1 whole, which is shorter than its diff:
```python
import functools

import jax
import jax.numpy as jnp
from jax import lax
from jax.experimental import pallas as pl
from jax.experimental.pallas import tpu as pltpu
from jax.sharding import PartitionSpec as P

MESH = pl.DeviceIdType.MESH
F32, BF = jnp.float32, jnp.bfloat16
HEAD_DIM = 64
EPS = 1e-05

ROWS, PAIRS, LEVELS = 256, 4, 6
COUNT = (256, 128, 64, 32, 16, 8)
AT = (0, 256, 384, 448, 480, 496)
STACK = 512
OWN = (32, 352, 544, 656)
LEFT = (16, 336, 528, 640, 704)
RIGHT = (288, 480, 608, 688, 720)
FAR = 736
KEYS = 768
BLANK = ((0, 16), (304, 32), (496, 32), (624, 16))
TILE_AT = (0, 64, 128, 192, 320, 384, 512, 640)
TILES = 8
HALO = 80


def nn(a, b):
    return lax.dot_general(a, b, (((1,), (0,)), ((), ())), preferred_element_type=F32)


def nt(a, b):
    return lax.dot_general(a, b, (((1,), (1,)), ((), ())), preferred_element_type=F32)


def tn(a, b):
    return lax.dot_general(a, b, (((0,), (0,)), ((), ())), preferred_element_type=F32)


def iota(shape, dim):
    return lax.broadcasted_iota(jnp.int32, shape, dim)


def level_counts(index, level, total, valid_len):
    factor = 1 << level
    c = jnp.clip(valid_len - index * factor, 0, factor)
    return jnp.where((index >= 0) & (index < total), c, 0).astype(F32)


def tile_weights(k, me, tensors, valid_len):
    i, j = iota((64, 128), 0), iota((64, 128), 1)
    if k < 7:
        level = 0 if k < 4 else 1 if k < 6 else 2
        first = 64 * (k - AT[level] // 64)
        n = COUNT[level]
        c = level_counts(me * n + first - 32 + j, level, n * tensors, valid_len)
        near = jnp.abs((i >> 4) - (j >> 4) + 2) <= 1
        if level:
            near = near & (jnp.abs((i >> 3) - (j >> 3) + 4) > 1)
        return jnp.where(near, c, 0.0)
    c3 = level_counts(me * 32 + j - 16, 3, 32 * tensors, valid_len)
    near3 = (jnp.abs((i >> 4) - (j >> 4) + 1) <= 1) & (jnp.abs((i >> 3) - (j >> 3) + 2) > 1)
    near3 = near3 & (i < 32) & (j < 64)
    key4 = jnp.where(j < 80, j - 80, j - 64)
    c4 = level_counts(me * 16 + key4, 4, 16 * tensors, valid_len)
    near4 = (jnp.abs(((i - 32) >> 3) - (key4 >> 3)) > 1) & (i >= 32) & (i < 48) & (j >= 64) & (j < 96)
    key5 = j - 96
    c5 = level_counts(key5, 5, 8 * tensors, valid_len)
    near5 = (jnp.abs(me - (key5 >> 3)) > 1) & (i >= 48) & (i < 56) & (j >= 96)
    return jnp.where(near3, c3, 0.0) + jnp.where(near4, c4, 0.0) + jnp.where(near5, c5, 0.0)


def row_divisors(me, tensors, valid_len):
    i = iota((STACK, 128), 0)
    out = jnp.ones((STACK, 128), F32)
    for level in range(1, LEVELS):
        c = level_counts(i - AT[level] + me * COUNT[level], level, COUNT[level] * tensors, valid_len)
        here = (i >= AT[level]) & (i < AT[level] + COUNT[level])
        out = jnp.where(here, 1.0 / jnp.maximum(c, 1.0), out)
    return out


def stack_factors():
    i = iota((STACK, 128), 0)
    out = jnp.full((STACK, 128), HEAD_DIM ** (-0.5), F32)
    for level in range(1, LEVELS):
        out = jnp.where(i >= AT[level], HEAD_DIM ** (-0.5) / (1 << level), out)
    return out


def pairs_of(ref, start, n):
    return ref[pl.ds(start, n, stride=2), :], ref[pl.ds(start + 1, n, stride=2), :]


def pool(ref):
    for level in range(LEVELS - 1):
        n = COUNT[level + 1]
        even, odd = pairs_of(ref, AT[level], n)
        ref[AT[level + 1] : AT[level + 1] + n, :] = even + odd


def doubled(ref, value, n):
    ref[pl.ds(0, n, stride=2), :] = value
    ref[pl.ds(1, n, stride=2), :] = value
    return ref[0 : 2 * n, :]


def normalised(v):
    centred = v - jnp.mean(v, axis=-1, keepdims=True)
    r = lax.rsqrt(jnp.mean(centred * centred, axis=-1, keepdims=True) + EPS)
    return centred * r, r


def norm_back(n, r, hg):
    return r * (hg - jnp.mean(hg, axis=-1, keepdims=True) - n * jnp.mean(hg * n, axis=-1, keepdims=True))


def gelu_both(u):
    c = 0.7978845608028654
    square = u * u
    th = jnp.tanh(c * (u + 0.044715 * (square * u)))
    half = 0.5 * (1.0 + th)
    slope = half + (0.5 * c) * u * (1.0 - th * th) * (1.0 + 0.134145 * square)
    return u * half, slope


def layer_kernel(
    tensors,
    len_ref,
    x_ref,
    cot_ref,
    wa_ref,
    wb_ref,
    out_ref,
    ingrad_ref,
    ga_ref,
    gb_ref,
    small_ref,
    qs,
    ks,
    vs,
    qb,
    kw,
    vw,
    wt,
    rdiv,
    edge_l,
    edge_r,
    halo_l,
    halo_r,
    far,
    eb,
    ns,
    ml,
    ds_,
    att,
    mm,
    tmp_a,
    tmp_b,
    tmp_c,
    n1s,
    n2s,
    dacc,
    us,
    mus,
    dqs,
    dkw,
    back_l,
    back_r,
    got_l,
    got_r,
    dfar,
    gfar,
    send_sem,
    recv_sem,
):
    me = lax.axis_index("tensor")
    valid_len = len_ref[0]
    barrier = pltpu.get_barrier_semaphore()
    for k in range(1, tensors):
        pl.semaphore_signal(barrier, inc=1, device_id={"tensor": lax.rem(me + k, tensors)}, device_id_type=MESH)
    pl.semaphore_wait(barrier, tensors - 1)

    lane = iota((64, 128), 1)
    low_lanes = lane < 64
    low_b = low_lanes.astype(F32).astype(BF)
    high_b = (1.0 - low_lanes.astype(F32)).astype(BF)

    def both(v):
        return jnp.concatenate([v * low_b, v * high_b], axis=0)

    def joined(v):
        return jnp.where(low_lanes, v[:64], v[64:])

    n1, r1 = normalised(x_ref[...].astype(F32))
    n1s[...] = n1
    n1b = n1.astype(BF)
    valid = (iota((ROWS, 128), 0) + me * ROWS < valid_len).astype(F32)
    for t in range(PAIRS):
        joint = nn(n1b[:, :256], wa_ref[t, 0]) + nn(n1b[:, 256:], wa_ref[t, 1])
        joint = joint.astype(BF).astype(F32)
        qs[t, 0:ROWS, :] = joint[:, :128]
        ks[t, 0:ROWS, :] = joint[:, 128:256] * valid
        vs[t, 0:ROWS, :] = joint[:, 256:] * valid
    rdiv[...] = row_divisors(me, tensors, valid_len)
    for k in range(TILES):
        wt[k] = tile_weights(k, me, tensors, valid_len)

    def pooling(p, carry):
        pool(qs.at[p])
        qs[p, 504:STACK, :] = jnp.zeros((8, 128), F32)
        qb[p] = (qs[p] * stack_factors()).astype(BF)
        for which, (raw, windows) in enumerate(((ks, kw), (vs, vw))):
            raw_p = raw.at[p]
            pool(raw_p)
            row = which * PAIRS + p
            for start, n in BLANK:
                windows[p, start : start + n, :] = jnp.zeros((n, 128), BF)
            for level in range(LEVELS - 1):
                n = COUNT[level]
                rows = slice(AT[level], AT[level] + n)
                coarse = (raw_p[rows, :] * rdiv[rows, :]).astype(BF)
                if level < 4:
                    windows[p, OWN[level] : OWN[level] + n, :] = coarse
                edge_l[row, 16 * level : 16 * level + 16, :] = coarse[:16]
                edge_r[row, 16 * level : 16 * level + 16, :] = coarse[n - 16 :]
            rows = slice(AT[5], AT[5] + 8)
            far[me, row] = raw_p[rows, :] * rdiv[rows, :]
        return carry

    lax.fori_loop(0, PAIRS, pooling, 0)

    def to_left(src, dst, sem):
        return pltpu.make_async_remote_copy(
            src, dst, send_sem.at[sem], recv_sem.at[sem], device_id={"tensor": jnp.maximum(me - 1, 0)}, device_id_type=MESH
        )

    def to_right(src, dst, sem):
        return pltpu.make_async_remote_copy(
            src,
            dst,
            send_sem.at[sem],
            recv_sem.at[sem],
            device_id={"tensor": jnp.minimum(me + 1, tensors - 1)},
            device_id_type=MESH,
        )

    def to_peer(k, src, dst, sem):
        return pltpu.make_async_remote_copy(
            src, dst, send_sem.at[sem], recv_sem.at[sem], device_id={"tensor": lax.rem(me + k, tensors)}, device_id_type=MESH
        )

    def exchange(base, left_src, left_dst, right_src, right_dst, far_src, far_dst):
        for k in range(1, tensors):
            to_peer(k, far_src(k), far_dst(k), base + 1 + k).start()

        @pl.when(me > 0)
        def _():
            to_left(left_src, left_dst, base).start()

        @pl.when(me < tensors - 1)
        def _():
            to_right(right_src, right_dst, base + 1).start()

    def exchanged(base, left_src, left_dst, right_src, right_dst, far_src, far_dst):
        @pl.when(me > 0)
        def _():
            to_left(left_src, left_dst, base).wait_send()
            to_right(right_src, right_dst, base + 1).wait_recv()

        @pl.when(me == 0)
        def _():
            right_dst[...] = jnp.zeros(right_dst.shape, BF)

        @pl.when(me < tensors - 1)
        def _():
            to_right(right_src, right_dst, base + 1).wait_send()
            to_left(left_src, left_dst, base).wait_recv()

        @pl.when(me == tensors - 1)
        def _():
            left_dst[...] = jnp.zeros(left_dst.shape, BF)

        for k in range(1, tensors):
            to_peer(k, far_src(k), far_dst(k), base + 1 + k).wait()

    halos = (0, edge_l, halo_r, edge_r, halo_l, lambda k: far.at[me], lambda k: far.at[me])
    exchange(*halos)
    exchanged(*halos)

    def attend(p, carry):
        for which, windows in enumerate((kw, vw)):
            row = which * PAIRS + p
            for level in range(LEVELS - 1):
                windows[p, LEFT[level] : LEFT[level] + 16, :] = halo_l[row, 16 * level : 16 * level + 16, :]
                windows[p, RIGHT[level] : RIGHT[level] + 16, :] = halo_r[row, 16 * level : 16 * level + 16, :]
            groups = jnp.concatenate([far[g, row] for g in range(tensors)], axis=0)
            windows[p, FAR:KEYS, :] = groups.astype(BF)
        for k in range(TILES):
            here = slice(64 * k, 64 * k + 64)
            keys = slice(TILE_AT[k], TILE_AT[k] + 128)
            s = nt(both(qb[p, here, :]), kw[p, keys, :])
            w = wt[k]
            w = jnp.concatenate([w, w], axis=0)
            s = jnp.where(w > 0.0, s, -1e30)
            m = jnp.max(s, axis=-1, keepdims=True)
            e = w * jnp.exp(s - m)
            low = e.astype(BF)
            total = jnp.sum(low.astype(F32), axis=-1, keepdims=True)
            eb[p, k] = low
            ns[here, :] = joined(nn(low, vw[p, keys, :]))
            ml[p, here, :] = joined(jnp.broadcast_to(m, (128, 128)))
            ds_[here, :] = joined(jnp.broadcast_to(total, (128, 128)))
        rows = slice(AT[5], AT[5] + 8)
        num, top, den = ns[rows, :], ml[p, rows, :], ds_[rows, :]
        for level in range(LEVELS - 2, -1, -1):
            n = COUNT[level]
            rows = slice(AT[level], AT[level] + n)
            num, top, den = doubled(tmp_a, num, n // 2), doubled(tmp_b, top, n // 2), doubled(tmp_c, den, n // 2)
            own = ml[p, rows, :]
            both_top = jnp.maximum(own, top)
            left, right = jnp.exp(own - both_top), jnp.exp(top - both_top)
            num = ns[rows, :] * left + num * right
            den = ds_[rows, :] * left + den * right
            top = both_top
        inverse = 1.0 / den
        att[p] = num * inverse
        mm[p] = top
        dacc[p] = inverse
        return carry

    lax.fori_loop(0, PAIRS, attend, 0)

    attb = [att[t].astype(BF) for t in range(PAIRS)]
    branch = []
    for y in range(2):
        total = nt(attb[0], wb_ref[0, y, :, 0:128])
        for t in range(1, PAIRS):
            total = total + nt(attb[t], wb_ref[t, y, :, 0:128])
        branch.append(total)
    branch = jnp.concatenate(branch, axis=1)
    middle = x_ref[...].astype(F32) + branch
    n2, r2 = normalised(middle)
    n2s[...] = n2
    n2b = n2.astype(BF)
    n2t = n2b.T
    cotb = cot_ref[...]
    cott = cotb.T

    dense, dn2 = [0.0, 0.0], [0.0, 0.0]
    for t in range(PAIRS):
        pre = nn(n2b[:, :256], wb_ref[t, 0, :, 128:640]) + nn(n2b[:, 256:], wb_ref[t, 1, :, 128:640])
        act, slope = gelu_both(pre)
        act = act.astype(BF)
        act_grad = nn(cotb[:, :256], wb_ref[t, 0, :, 640:1152]) + nn(cotb[:, 256:], wb_ref[t, 1, :, 640:1152])
        pre_grad = (act_grad * slope).astype(BF)
        for y in range(2):
            half = slice(256 * y, 256 * y + 256)
            dense[y] = dense[y] + nt(act, wb_ref[t, y, :, 640:1152])
            dn2[y] = dn2[y] + nt(pre_grad, wb_ref[t, y, :, 128:640])
            gb_ref[t, y, :, 128:640] = nn(n2t[half, :], pre_grad).astype(BF)
            gb_ref[t, y, :, 640:1152] = nn(cott[half, :], act).astype(BF)
    dense = jnp.concatenate(dense, axis=1)
    dn2 = jnp.concatenate(dn2, axis=1)
    result = middle + dense
    out_ref[...] = result.astype(BF)
    live = (iota((ROWS, 512), 0) + me * ROWS < valid_len).astype(F32)
    small_ref[2:3, :] = jnp.sum(live * result * result, axis=0, keepdims=True)
    small_ref[3:4, :] = jnp.sum(live * branch * branch, axis=0, keepdims=True)
    small_ref[4:5, :] = jnp.sum(live * dense * dense, axis=0, keepdims=True)
    small_ref[5:6, :] = jnp.sum(live, axis=0, keepdims=True)
    small_ref[6:8, :] = jnp.zeros((2, 512), F32)
    n2 = n2s[...]
    small_ref[1:2, :] = jnp.sum(dn2 * n2, axis=0, keepdims=True)
    middle_grad = cotb.astype(F32) + norm_back(n2, r2, dn2)
    n2s[...] = middle_grad
    mgb = middle_grad.astype(BF)
    mgt = mgb.T
    for t in range(PAIRS):
        us[t, 0:ROWS, :] = nn(mgb[:, :256], wb_ref[t, 0, :, 0:128]) + nn(mgb[:, 256:], wb_ref[t, 1, :, 0:128])
        for y in range(2):
            gb_ref[t, y, :, 0:128] = nn(mgt[256 * y : 256 * y + 256, :], att[t].astype(BF)).astype(BF)

    def head_sums(v):
        first = jnp.sum(jnp.where(iota(v.shape, 1) < 64, v, 0.0), axis=-1, keepdims=True)
        second = jnp.sum(jnp.where(iota(v.shape, 1) < 64, 0.0, v), axis=-1, keepdims=True)
        return jnp.where(iota(v.shape, 1) < 64, first, second)

    def attend_back(p, carry):
        up = us.at[p]
        grad, inverse = up[0:ROWS, :], dacc[p]
        delta = head_sums(grad * att[p])
        up[0:ROWS, :] = grad * inverse
        ns[0:ROWS, :] = delta * inverse
        mus[0:ROWS, :] = mm[p]
        for level in range(LEVELS - 1):
            n = COUNT[level + 1]
            after = slice(AT[level + 1], AT[level + 1] + n)
            top_e, top_o = pairs_of(mus, AT[level], n)
            top = jnp.minimum(top_e, top_o)
            fe, fo = jnp.exp(top - top_e), jnp.exp(top - top_o)
            u_e, u_o = pairs_of(up, AT[level], n)
            d_e, d_o = pairs_of(ns, AT[level], n)
            up[after, :] = u_e * fe + u_o * fo
            ns[after, :] = d_e * fe + d_o * fo
            mus[after, :] = top
        for rows in (slice(504, STACK),):
            up[rows, :] = jnp.zeros((8, 128), F32)
            ns[rows, :] = jnp.zeros((8, 128), F32)
            mus[rows, :] = jnp.zeros((8, 128), F32)
        for which in range(2):
            dkw[which * PAIRS + p, 0:512, :] = jnp.zeros((512, 128), F32)
        for k in range(TILES):
            here = slice(64 * k, 64 * k + 64)
            keys = slice(TILE_AT[k], TILE_AT[k] + 128)
            factor = jnp.exp(ml[p, here, :] - mus[here, :])
            g = up[here, :] * factor
            g_high = g.astype(BF)
            g2 = both(g_high)
            g4 = jnp.concatenate([g2, both((g - g_high.astype(F32)).astype(BF))], axis=1)
            v2 = vw[p, keys, :]
            v2 = jnp.concatenate([v2, v2], axis=1)
            h = ns[here, :] * factor
            h2 = jnp.concatenate([h[:, 0:1], h[:, 64:65]], axis=0)
            q2 = both(qb[p, here, :])
            low = eb[p, k]
            d = low.astype(F32) * (nt(g4, v2) - h2)
            d = d.astype(BF)
            dv = tn(low, g2)
            dk = tn(d, q2)
            if k < 6:
                dkw[p, keys, :] = dkw[p, keys, :] + dk
                dkw[PAIRS + p, keys, :] = dkw[PAIRS + p, keys, :] + dv
            else:
                dkw[p, keys, :] = dk
                dkw[PAIRS + p, keys, :] = dv
            dqs[p, here, :] = joined(nn(d, kw[p, keys, :]))
        for which in range(2):
            row = which * PAIRS + p
            for level in range(LEVELS - 1):
                part = slice(16 * level, 16 * level + 16)
                back_l[row, part, :] = dkw[row, LEFT[level] : LEFT[level] + 16, :].astype(BF)
                back_r[row, part, :] = dkw[row, RIGHT[level] : RIGHT[level] + 16, :].astype(BF)
            for g in range(tensors):
                dfar[g, row] = dkw[row, FAR + 8 * g : FAR + 8 * g + 8, :]
        return carry

    lax.fori_loop(0, PAIRS, attend_back, 0)

    back = (
        8,
        back_l,
        got_r,
        back_r,
        got_l,
        lambda k: dfar.at[lax.rem(me + k, tensors)],
        lambda k: gfar.at[k],
    )
    exchange(*back)
    exchanged(*back)

    def unpool(p, carry):
        factors = stack_factors()
        cur = dqs[p, AT[5] : AT[5] + 8, :] * factors[AT[5] : AT[5] + 8]
        for level in range(LEVELS - 2, -1, -1):
            rows = slice(AT[level], AT[level] + COUNT[level])
            cur = doubled(tmp_a, cur, COUNT[level] // 2) + dqs[p, rows, :] * factors[rows]
        qs[p, 0:ROWS, :] = cur
        for which, raw in enumerate((ks, vs)):
            row = which * PAIRS + p
            raw_p = raw.at[p]
            cur = gfar[1, row]
            for k in range(2, tensors):
                cur = cur + gfar[k, row]
            cur = cur * rdiv[AT[5] : AT[5] + 8, :]
            for level in range(LEVELS - 2, -1, -1):
                n = COUNT[level]
                rows = slice(AT[level], AT[level] + n)
                part = slice(16 * level, 16 * level + 16)
                if level < 4:
                    raw_p[rows, :] = dkw[row, OWN[level] : OWN[level] + n, :]
                else:
                    raw_p[rows, :] = jnp.zeros((n, 128), F32)
                first = slice(AT[level], AT[level] + 16)
                last = slice(AT[level] + n - 16, AT[level] + n)
                raw_p[first, :] = raw_p[first, :] + got_l[row, part, :].astype(F32)
                raw_p[last, :] = raw_p[last, :] + got_r[row, part, :].astype(F32)
                cur = doubled(tmp_a, cur, n // 2) + raw_p[rows, :] * rdiv[rows, :]
            raw_p[0:ROWS, :] = cur * (iota((ROWS, 128), 0) + me * ROWS < valid_len).astype(F32)
        return carry

    lax.fori_loop(0, PAIRS, unpool, 0)

    n1 = n1s[...]
    n1t = n1.astype(BF).T
    dn1 = [0.0, 0.0]
    for t in range(PAIRS):
        joint = jnp.concatenate(
            [qs[t, 0:ROWS, :].astype(BF), ks[t, 0:ROWS, :].astype(BF), vs[t, 0:ROWS, :].astype(BF)], axis=1
        )
        for y in range(2):
            ga_ref[t, y] = nn(n1t[256 * y : 256 * y + 256, :], joint).astype(BF)
            dn1[y] = dn1[y] + nt(joint, wa_ref[t, y])
    dn1 = jnp.concatenate(dn1, axis=1)
    small_ref[0:1, :] = jnp.sum(dn1 * n1, axis=0, keepdims=True)
    r1 = lax.rsqrt(row_variance(x_ref[...].astype(F32)) + EPS)
    ingrad_ref[...] = (n2s[...] + norm_back(n1, r1, dn1)).astype(BF)


def row_variance(v):
    centred = v - jnp.mean(v, axis=-1, keepdims=True)
    return jnp.mean(centred * centred, axis=-1, keepdims=True)


def run_layer(tensors, lengths, inputs, cotangent, wa, wb):
    vmem = pl.BlockSpec(memory_space=pltpu.VMEM)
    f = lambda *shape: pltpu.VMEM(shape, F32)
    b = lambda *shape: pltpu.VMEM(shape, BF)
    return pl.pallas_call(
        functools.partial(layer_kernel, tensors),
        out_shape=(
            jax.ShapeDtypeStruct((ROWS, 512), BF),
            jax.ShapeDtypeStruct((ROWS, 512), BF),
            jax.ShapeDtypeStruct(wa.shape, BF),
            jax.ShapeDtypeStruct(wb.shape, BF),
            jax.ShapeDtypeStruct((8, 512), F32),
        ),
        in_specs=[pl.BlockSpec(memory_space=pltpu.SMEM), vmem, vmem, vmem, vmem],
        out_specs=(vmem,) * 5,
        scratch_shapes=[
            f(PAIRS, STACK, 128),
            f(PAIRS, STACK, 128),
            f(PAIRS, STACK, 128),
            b(PAIRS, STACK, 128),
            b(PAIRS, KEYS, 128),
            b(PAIRS, KEYS, 128),
            f(TILES, 64, 128),
            f(STACK, 128),
            b(2 * PAIRS, HALO, 128),
            b(2 * PAIRS, HALO, 128),
            b(2 * PAIRS, HALO, 128),
            b(2 * PAIRS, HALO, 128),
            f(tensors, 2 * PAIRS, 8, 128),
            b(PAIRS, TILES, 128, 128),
            f(STACK, 128),
            f(PAIRS, STACK, 128),
            f(STACK, 128),
            f(PAIRS, ROWS, 128),
            f(PAIRS, ROWS, 128),
            f(ROWS, 128),
            f(ROWS, 128),
            f(ROWS, 128),
            f(ROWS, 512),
            f(ROWS, 512),
            f(PAIRS, ROWS, 128),
            f(PAIRS, STACK, 128),
            f(STACK, 128),
            f(PAIRS, STACK, 128),
            f(2 * PAIRS, KEYS, 128),
            b(2 * PAIRS, HALO, 128),
            b(2 * PAIRS, HALO, 128),
            b(2 * PAIRS, HALO, 128),
            b(2 * PAIRS, HALO, 128),
            f(tensors, 2 * PAIRS, 8, 128),
            f(tensors, 2 * PAIRS, 8, 128),
            pltpu.SemaphoreType.DMA((16,)),
            pltpu.SemaphoreType.DMA((16,)),
        ],
        compiler_params=pltpu.CompilerParams(
            collective_id=0, has_side_effects=True, vmem_limit_bytes=60 * 1024 * 1024
        ),
        name="layer",
    )(lengths, inputs, cotangent, wa, wb)


def per_device(
    inputs,
    lengths,
    cotangent,
    query_weight,
    key_weight,
    value_weight,
    output_weight,
    inner_weight,
    outer_weight,
    first_gain,
    second_gain,
):
    tensors, groups = lax.axis_size("tensor"), lax.axis_size("dp")
    everyone = ("tensor", "dp")
    g1 = first_gain.astype(F32)[:, None]
    g2 = second_gain.astype(F32)[:, None]
    scaled = lambda g, w: (g * w.astype(F32)).astype(BF)
    part_a = scaled(g1, jnp.concatenate([query_weight, key_weight, value_weight], axis=1))
    part_b = jnp.concatenate([output_weight.T, scaled(g2, inner_weight), outer_weight.T], axis=1)
    wa = lax.all_gather(part_a, everyone, axis=0, tiled=True).reshape(tensors, 2, 256, 384)
    wb = lax.all_gather(part_b, everyone, axis=0, tiled=True).reshape(tensors, 2, 256, 1152)
    out, input_grad, ga, gb, small = run_layer(tensors, lengths, inputs, cotangent, wa, wb)
    width = first_gain.shape[0]

    def reduced(g):
        return lax.psum_scatter(
            g.reshape(tensors * 512, g.shape[-1]).astype(F32), everyone, scatter_dimension=0, tiled=True
        )

    ga, gb, small = reduced(ga), reduced(gb), lax.psum(small, everyone)
    at = lax.axis_index("dp") * width
    gains = lax.dynamic_slice(small, (0, at), (2, width))
    sums = jnp.sum(small, axis=1)
    root_mean_squares = jnp.sqrt(sums[2:5] / sums[5])
    ga = ga * g1
    return (
        out,
        input_grad,
        ga[:, 0:128],
        ga[:, 128:256],
        ga[:, 256:384],
        gb[:, 0:128].T,
        gb[:, 128:640] * g2,
        gb[:, 640:1152].T,
        gains[0] / first_gain.astype(F32),
        gains[1] / second_gain.astype(F32),
        root_mean_squares,
    )


def solution(mesh):
    return jax.shard_map(
        per_device,
        mesh=mesh,
        in_specs=(
            P(("dp", "tensor"), None),
            P("dp"),
            P(("dp", "tensor"), None),
            P("dp", "tensor"),
            P("dp", "tensor"),
            P("dp", "tensor"),
            P("tensor", "dp"),
            P("dp", "tensor"),
            P("tensor", "dp"),
            P("dp"),
            P("dp"),
        ),
        out_specs=(
            P(("dp", "tensor"), None),
            P(("dp", "tensor"), None),
            P("dp", "tensor"),
            P("dp", "tensor"),
            P("dp", "tensor"),
            P("tensor", "dp"),
            P("dp", "tensor"),
            P("tensor", "dp"),
            P("dp"),
            P("dp"),
            P(),
        ),
        check_vma=False,
    )
```

time: 775 us -> 431 us (0.56)
  waiting for transfers between devices: 87.9 us -> 313 us
  blocking collectives: 254 us -> 40.4 us
  local copies, waits for them, and re-layouts: 148 us -> 4.76 us
  other arithmetic: 130 us -> 19.6 us
  matrix products: 107 us -> 0 us
  Pallas kernels: 0 us -> 38.6 us
  starting transfers between devices: 19.2 us -> 0.16 us
    all_gather x6 -> x0, blocking collectives: 192 us -> none  [the longest x1 34 us: per_device(): lax.all_gather(outer_weight, 'dp', axis=1, tiled=True)]
    reduce_scatter x4 -> x2, waiting for transfers between devices: 65.9 us -> 191 us  [reduced(): lax.psum_scatter(g.reshape(tensors * 512, g.shape[-1]).astype(F32), every...]
    all_gather x4 -> x2, waiting for transfers between devices: 0.03 us -> 122 us  [the longest x1 65.9 us: per_device(): lax.all_gather(part_b, everyone, axis=0, tiled=True)]
    dot_general x48 -> x0, matrix products: 107 us -> none  [the longest x18 39.5 us: level_terms(): jnp.einsum('vwg,vgi->vwi', weighted_values, nearby_value_rows, precision=...]
    reduce_sum x48 -> x1, other arithmetic: 80.3 us -> 0.12 us  [per_device(): sums = jnp.sum(small, axis=1)]
    reshape x62 -> x0, local copies, waits for them, and re-layouts: 52.6 us -> none  [the longest x20 20.7 us: level_terms(): jnp.repeat(row_top, factor)]
    pallas_call x0 -> x1, Pallas kernels: none -> 38.6 us  [run_layer(): pl.pallas_call(functools.partial(layer_kernel, tensors), out_shape=(jax.S...]
    reduce_sum x39 -> x0, local copies, waits for them, and re-layouts: 28.4 us -> none  [the longest x25 25.4 us: hierarchy(): softmax_numerator = softmax_numerator + entry[0] * factor_now[:, None]]
  transfers between devices with their start and end apart: 12 -> 4, of which waited for: 6 -> 4; matrix products, arithmetic and copies ran while one was open for 32% -> 3% of each run, Pallas kernels for 0% -> 0%
where the time goes in v1:
time: 431 us
  waiting for transfers between devices  313 us (73%)
  blocking collectives  40.4 us (9%)
  Pallas kernels  38.6 us (9%)
  other arithmetic  19.6 us (5%)
  between operations  14.5 us (3%)
  local copies, waits for them, and re-layouts  4.76 us (1%)
    reduce_scatter x2, waiting for transfers between devices, reduced(): lax.psum_scatter(g.reshape(tensors * 512, g.shape[-1]).astype(F32), every...  191 us
    all_gather x1, waiting for transfers between devices, per_device(): lax.all_gather(part_b, everyone, axis=0, tiled=True)  65.9 us
    all_gather x1, waiting for transfers between devices, per_device(): lax.all_gather(part_a, everyone, axis=0, tiled=True)  56 us
    psum x1, blocking collectives, per_device(): ga, gb, small = (reduced(ga), reduced(gb), lax.psum(small, everyone))  40.4 us
    pallas_call x1, Pallas kernels, run_layer(): pl.pallas_call(functools.partial(layer_kernel, tensors), out_shape=(jax.S...  38.6 us
    convert_element_type x2, other arithmetic, reduced(): g.reshape(tensors * 512, g.shape[-1]).astype(F32)  9.81 us
  transfers between devices with their start and end apart: 4, of which 4 were waited for; matrix products, arithmetic and copies ran while one was open for 3% of the time, Pallas kernels for 0%

profile of v1, /device:TPU:0, one launch (start us, length us, event | category | flops | bytes accessed | tf_op | source)
XLA Modules:
  0.0 430.8 jit_solution(14034614550224709895)
XLA Ops:
  7.2 0.0 all-gather.3.cloned.1.call-start
  7.2 0.7 convert_element_type.32
  7.9 1.4 multiply_convert_fusion.1
  9.3 0.0 all-gather.3.cloned.1.call-update
  9.4 0.0 all-gather.5.cloned.1.call-start
  9.4 0.7 convert_element_type.35
  10.1 0.9 multiply_convert_fusion
  11.0 1.5 pad_maximum_fusion
  12.5 0.0 reduce-scatter.3.cloned.1.call-start
  13.2 56.0 %all-gather.3.cloned.1.call-done = bf16[2048,384]{1,0:T(8,128)(2,1)} async-done(((bf16[64,384]{1,0:T(8,128)(2,1)}), bf16[2048,384]{1,0:T(8,128)(2,1)}) %all-gather.3.cloned.1.call-update) | async-done | bytes 1572880 | tf_op jit(solution)/shard_map/all_gather | solution.py:598
  69.3 65.9 %all-gather.5.cloned.1.call-done = bf16[2048,1152]{1,0:T(8,128)(2,1)} async-done(((bf16[64,1152]{1,0:T(8,128)(2,1)}), bf16[2048,1152]{1,0:T(8,128)(2,1)}) %all-gather.5.cloned.1.call-update) | async-done | bytes 4718608 | tf_op jit(solution)/shard_map/all_gather | solution.py:599
  135.2 38.6 %layer.1 = (bf16[256,512]{1,0:T(8,128)(2,1)}, bf16[256,512]{1,0:T(8,128)(2,1)}, bf16[4,2,256,384]{3,2,1,0:T(8,128)(2,1)}, bf16[4,2,256,1152]{3,2,1,0:T(8,128)(2,1)}, f32[8,512]{1,0:T(8,128)}) custom-call(s32[1]{0:T(128)S(6)} %copy.24.len_ref, bf16[256,512]{1,0:T(8,128)(2,1)} %x_ref.1, bf16[256,512]{1,0:T(8,128)(2,1)} %cot_ref.1, ...), custom_call_target="tpu_custom_call" | custom-call | tf_op jit(solution)/shard_map/layer/pallas_call | solution.py:521
  173.8 3.2 bitcast_convert_fusion.1
  177.1 0.0 reduce-scatter.3.cloned.1.call-update
  177.1 0.0 reduce-scatter.5.cloned.1.call-start
  177.1 6.6 %bitcast_convert_fusion = f32[2048,1152]{1,0:T(8,128)} fusion(bf16[4,2,256,1152]{3,2,1,0:T(8,128)(2,1)} %get-tuple-element.19), kind=kLoop, calls=%fused_computation | loop fusion | flops 2359296 | bytes 14155776 | tf_op jit(solution)/shard_map/convert_element_type | solution.py:605
  183.7 0.0 reduce-scatter.5.cloned.1.call-update
  183.8 0.7 copy-done.2
  184.4 40.4 %psum.7 = f32[8,512]{1,0:T(8,128)S(1)} all-reduce(f32[8,512]{1,0:T(8,128)S(1)} %copy-done.2), channel_id=1, replica_groups=mesh['dp'=8,'tensor'=4] {'tensor','dp'}, use_global_device_ids=true, to_apply=%region_2.0 | all-reduce | flops 4096 | bytes 32768 | tf_op jit(solution)/shard_map/psum | solution.py:608
  224.8 0.1 reduce_sum.9
  225.0 0.6 slice.39
  225.5 0.1 constant_dynamic-slice_fusion
  225.6 1.2 divide_sqrt_fusion
  226.9 0.5 bitcast_divide_fusion
  227.4 51.5 %reduce-scatter.3.cloned.1.call-done = f32[64,384]{1,0:T(8,128)} async-done(((f32[2048,384]{1,0:T(8,128)}), f32[64,384]{1,0:T(8,128)}) %reduce-scatter.3.cloned.1.call-update) | async-done | bytes 98320 | tf_op jit(solution)/shard_map/reduce_scatter | solution.py:604
  278.9 1.0 broadcast_multiply_fusion
  279.9 0.6 fusion
  280.5 139.3 %reduce-scatter.5.cloned.1.call-done = f32[64,1152]{1,0:T(8,128)} async-done(((f32[2048,1152]{1,0:T(8,128)}), f32[64,1152]{1,0:T(8,128)}) %reduce-scatter.5.cloned.1.call-update) | async-done | bytes 294928 | tf_op jit(solution)/shard_map/reduce_scatter | solution.py:604
  419.8 1.4 slice_bitcast_fusion.1
  421.2 1.7 slice_bitcast_fusion
  422.9 0.7 copy.25
  423.6 0.7 copy.26
  (10 shorter events, 0.0 us)
Async XLA Ops:
  7.2 62.1 %all-gather.3.cloned.1.call-start = ((), (), s32[]{:S(2)}) async-start(), calls=%async_computation.2 | async-start | bytes 1622016 | tf_op jit(solution)/shard_map/all_gather | solution.py:598
  9.4 125.8 %all-gather.5.cloned.1.call-start = ((), (), s32[]{:S(2)}) async-start(), calls=%async_computation.3 | async-start | bytes 4866048 | tf_op jit(solution)/shard_map/all_gather | solution.py:599
  12.5 266.4 %reduce-scatter.3.cloned.1.call-start = ((), (), s32[]{:S(2)}) async-start(), calls=%async_computation.4 | async-start | bytes 3244032 | tf_op jit(solution)/shard_map/reduce_scatter | solution.py:604
  177.1 242.7 %reduce-scatter.5.cloned.1.call-start = ((), (), s32[]{:S(2)}) async-start(), calls=%async_computation.5 | async-start | bytes 9732096 | tf_op jit(solution)/shard_map/reduce_scatter | solution.py:604
  183.7 0.7 copy-start.2
  183.7 43.1 %copy-start.3 = (bf16[64]{0:T(256)(128)(2,1)S(1)}, bf16[64]{0:T(256)(128)(2,1)}, u32[]{:S(2)}) copy-start(bf16[64]{0:T(256)(128)(2,1)} %param.20) | copy-start | bytes 388
  183.7 43.1 %copy-start.4 = (bf16[64]{0:T(256)(128)(2,1)S(1)}, bf16[64]{0:T(256)(128)(2,1)}, u32[]{:S(2)}) copy-start(bf16[64]{0:T(256)(128)(2,1)} %param.21) | copy-start | bytes 388
  183.7 239.2 %copy-start.1 = (bf16[256,512]{1,0:T(8,128)(2,1)S(1)}, bf16[256,512]{1,0:T(8,128)(2,1)}, u32[]{:S(2)}) copy-start(bf16[256,512]{1,0:T(8,128)(2,1)} %get-tuple-element.39) | copy-start | bytes 786436
  183.7 239.9 %copy-start = (bf16[256,512]{1,0:T(8,128)(2,1)S(1)}, bf16[256,512]{1,0:T(8,128)(2,1)}, u32[]{:S(2)}) copy-start(bf16[256,512]{1,0:T(8,128)(2,1)} %get-tuple-element.40) | copy-start | bytes 786436
Sparse Core Ops, SparseCore 0:
  11.5 57.7 all-gather.2
  72.7 62.4 all-gather.4
  177.2 101.6 reduce-scatter.2
  284.6 135.1 reduce-scatter.4

commit v2 on v1

--- a/solution.py
+++ b/solution.py
@@ -126,62 +126,240 @@
     return u * half, slope
 
 
-def layer_kernel(
-    tensors,
-    len_ref,
-    x_ref,
-    cot_ref,
-    wa_ref,
-    wb_ref,
-    out_ref,
-    ingrad_ref,
-    ga_ref,
-    gb_ref,
-    small_ref,
-    qs,
-    ks,
-    vs,
-    qb,
-    kw,
-    vw,
-    wt,
-    rdiv,
-    edge_l,
-    edge_r,
-    halo_l,
-    halo_r,
-    far,
-    eb,
-    ns,
-    ml,
-    ds_,
-    att,
-    mm,
-    tmp_a,
-    tmp_b,
-    tmp_c,
-    n1s,
-    n2s,
-    dacc,
-    us,
-    mus,
-    dqs,
-    dkw,
-    back_l,
-    back_r,
-    got_l,
-    got_r,
-    dfar,
-    gfar,
-    send_sem,
-    recv_sem,
-):
+class Place:
+    def __init__(self):
+        self.d, self.t = lax.axis_index("dp"), lax.axis_index("tensor")
+        self.z, self.y = self.d // 2, self.d % 2
+        self.x, self.c = self.t // 2, self.t % 2
+        self.a = self.x + self.c * (self.y - self.x)
+        self.b = self.y + self.c * (self.x - self.y)
+        flip_x, flip_y = 2 - 4 * self.x, 1 - 2 * self.y
+        self.to_x, self.to_y = (self.d, self.t + flip_x), (self.d + flip_y, self.t)
+        self.to_a = (self.d + self.c * flip_y, self.t + (1 - self.c) * flip_x)
+        self.to_b = (self.d + (1 - self.c) * flip_y, self.t + self.c * flip_x)
+        self.to_other = (self.d, self.t + 1 - 2 * self.c)
+        self.to_across = (self.d, 3 - self.t)
+
+    def to_z(self, k):
+        return (2 * ((self.z + k) % 4) + self.y, self.t)
+
+
+def flipped(bit, by):
+    return 1 - bit if by else bit
+
+
+class Remote:
+    def __init__(self, send_sem, recv_sem):
+        self.send_sem, self.recv_sem, self.started = send_sem, recv_sem, set()
+
+    def copy(self, i, src, dst, to):
+        return pltpu.make_async_remote_copy(
+            src, dst, self.send_sem.at[i], self.recv_sem.at[i], device_id=to, device_id_type=MESH
+        )
+
+    def send(self, i, src, dst, to):
+        self.copy(i, src, dst, to).start()
+        self.started.add(i)
+
+    def arrived(self, i, dst, to):
+        self.copy(i, dst, dst, to).wait_recv()
+
+    def drain(self, like, to):
+        for i in sorted(self.started):
+            self.copy(i, like, like, to).wait_send()
+
+
+class Gather(Remote):
+    def __init__(self, at, own, w, send_sem, recv_sem):
+        super().__init__(send_sem, recv_sem)
+        self.at, self.own, self.w = at, own, w
+
+    def shard(self, j, aa=0, bb=0, plane=0):
+        at = self.at
+        a, b = (at.b, at.a) if plane else (at.a, at.b)
+        return self.w.at[flipped(at.c, plane), flipped(a, aa), flipped(b, bb), (at.z + 4 - j) % 4]
+
+    def source(self, j, aa=0, bb=0):
+        return self.own if (j, aa, bb) == (0, 0, 0) else self.shard(j, aa, bb)
+
+    def along_z(self):
+        for k in (1, 3, 2):
+            self.send(k - 1, self.own, self.shard(0), self.at.to_z(k))
+
+    def along_b(self, j):
+        self.send(3 + j, self.source(j), self.shard(j), self.at.to_b)
+
+    def along_a(self, j, bb):
+        self.send(7 + 4 * bb + j, self.source(j, 0, bb), self.shard(j, 0, bb), self.at.to_a)
+
+    def across(self, j, aa, bb):
+        self.send(15 + 8 * aa + 4 * bb + j, self.source(j, aa, bb), self.shard(j, aa, bb), self.at.to_other)
+
+    def own_on(self):
+        self.along_b(0)
+        self.along_a(0, 0)
+        self.across(0, 0, 0)
+
+    def after_z(self):
+        for j in (1, 3, 2):
+            self.arrived(j - 1, self.shard(j), self.at.to_b)
+            self.along_b(j)
+            self.along_a(j, 0)
+            self.across(j, 0, 0)
+
+    def after_b(self):
+        for j in (0, 1, 3, 2):
+            self.arrived(3 + j, self.shard(j, 0, 1), self.at.to_b)
+            self.along_a(j, 1)
+            self.across(j, 0, 1)
+
+    def after_a(self, bb):
+        for j in (0, 1, 3, 2):
+            self.arrived(7 + 4 * bb + j, self.shard(j, 1, bb), self.at.to_b)
+            self.across(j, 1, bb)
+
+    def after_across(self):
+        for aa in range(2):
+            for bb in range(2):
+                for j in range(4):
+                    self.arrived(15 + 8 * aa + 4 * bb + j, self.shard(j, aa, bb, 1), self.at.to_b)
+
+
+class Reduce(Remote):
+    def __init__(self, at, g, r0, r1, r2, r3, send_sem, recv_sem):
+        super().__init__(send_sem, recv_sem)
+        self.at, self.g, self.r0, self.r1, self.r2, self.r3 = at, g, r0, r1, r2, r3
+
+    def across(self, t, lo, hi, base):
+        @pl.when(self.at.c != t % 2)
+        def _():
+            for a, b in ((t // 2, 0), (t // 2, 1)) if t % 2 == 0 else ((0, t // 2), (1, t // 2)):
+                self.copy(
+                    base + 2 * a + b,
+                    self.g.at[t % 2, a, b, :, :, lo:hi],
+                    self.r0.at[a, b, :, :, lo:hi],
+                    self.at.to_other,
+                ).start()
+
+    def across_wait(self, a, b, lo, hi, base):
+        piece = self.r0.at[a, b, :, :, lo:hi]
+        copy = self.copy(base + 2 * a + b, piece, piece, self.at.to_other)
+        copy.wait_recv()
+
+    def across_drain(self, lo, hi, base):
+        for i in range(4):
+            piece = self.r0.at[i // 2, i % 2, :, :, lo:hi]
+            self.copy(base + i, piece, piece, self.at.to_other).wait_send()
+
+    def far_half(self, parts):
+        at = self.at
+        for bb in (1, 0):
+            b = flipped(at.b, bb)
+            for lo, hi, base in parts:
+                self.across_wait(1 - at.a, b, lo, hi, base)
+            for j in range(4):
+                z = (at.z + j) % 4
+                here = self.g.at[at.c, 1 - at.a, b, z]
+                here[...] = (here[...].astype(F32) + self.r0[1 - at.a, b, z].astype(F32)).astype(BF)
+                self.send(8 + 4 * bb + j, here, self.r1.at[b, z], at.to_a)
+
+    def near_half(self, parts):
+        at = self.at
+        b = 1 - at.b
+        for lo, hi, base in parts:
+            self.across_wait(at.a, b, lo, hi, base)
+        for j in range(4):
+            z = (at.z + j) % 4
+            here = self.g.at[at.c, at.a, b, z]
+            self.arrived(12 + j, self.r1.at[b, z], at.to_a)
+            total = here[...].astype(F32) + self.r0[at.a, b, z].astype(F32) + self.r1[b, z].astype(F32)
+            here[...] = total.astype(BF)
+            self.send(16 + j, here, self.r2.at[z], at.to_b)
+
+    def own_quarter(self, parts, out):
+        at = self.at
+        b = at.b
+        for lo, hi, base in parts:
+            self.across_wait(at.a, b, lo, hi, base)
+        for j in (1, 3, 2, 0):
+            z = (at.z + j) % 4
+            here = self.g.at[at.c, at.a, b, z]
+            self.arrived(8 + j, self.r1.at[b, z], at.to_a)
+            self.arrived(16 + j, self.r2.at[z], at.to_b)
+            total = here[...].astype(F32) + self.r0[at.a, b, z].astype(F32)
+            total = total + self.r1[b, z].astype(F32) + self.r2[z].astype(F32)
+            if j:
+                here[...] = total.astype(BF)
+                self.send(20 + j - 1, here, self.r3.at[j - 1], at.to_z(j))
+            else:
+                out[...] = total
+
+    def finish(self, out):
+        for k in (1, 3, 2):
+            self.arrived(20 + k - 1, self.r3.at[k - 1], self.at.to_b)
+        total = out[...] + self.r3[0].astype(F32)
+        out[...] = total + self.r3[1].astype(F32) + self.r3[2].astype(F32)
+
+
+def mixed(v, into):
+    tiles = [v[:, 128 * i : 128 * i + 128] for i in range(4)]
+    rolled = [pltpu.roll(tile, 64, 1) for tile in tiles]
+    low = iota(tiles[0].shape, 1) < 64
+    if into:
+        pairs = ((0, 1, 0), (2, 3, 0), (0, 1, 1), (2, 3, 1))
+    else:
+        pairs = ((0, 2, 0), (0, 2, 1), (1, 3, 0), (1, 3, 1))
+    out = []
+    for i, k, high in pairs:
+        out.append(jnp.where(low, rolled[i], tiles[k]) if high else jnp.where(low, tiles[i], rolled[k]))
+    return jnp.concatenate(out, axis=1)
+
+
+def layer_kernel(fast, tensors, names, *refs):
+    ref = dict(zip(names, refs, strict=True))
+    len_ref, x_ref, cot_ref, out_ref, ingrad_ref = (ref[n] for n in ("lengths", "x", "cot", "out", "ingrad"))
+    qs, ks, vs, qb, kw, vw, wt, rdiv = (ref[n] for n in ("qs", "ks", "vs", "qb", "kw", "vw", "wt", "rdiv"))
+    edge_l, edge_r, halo_l, halo_r, far = (ref[n] for n in ("edge_l", "edge_r", "halo_l", "halo_r", "far"))
+    eb, ns, ml, ds_, att, mm = (ref[n] for n in ("eb", "ns", "ml", "ds", "att", "mm"))
+    tmp_a, tmp_b, tmp_c, n1s, n2s, dacc = (ref[n] for n in ("tmp_a", "tmp_b", "tmp_c", "n1s", "n2s", "dacc"))
+    us, mus, dqs, dkw = (ref[n] for n in ("us", "mus", "dqs", "dkw"))
+    back_l, back_r, got_l, got_r, dfar, gfar = (
+        ref[n] for n in ("back_l", "back_r", "got_l", "got_r", "dfar", "gfar")
+    )
+    send_sem, recv_sem, small_ref = ref["send_sem"], ref["recv_sem"], ref["small"]
+    ga, gb = ref["ga"], ref["gb"]
+    wa, wb = (ref["wa"], ref["wb"])
+
+    def view(r, t, y):
+        if not fast:
+            return r.at[t, y]
+        return r.at[0, t // 2, y] if t % 2 == 0 else r.at[1, y, t // 2]
+
+    def get(r, t, y, lo, hi):
+        return view(r, t, y)[..., lo:hi].reshape(256, hi - lo)
+
+    def put(r, t, y, lo, hi, value):
+        v = view(r, t, y)
+        v[..., lo:hi] = value.astype(BF).reshape(*v.shape[:-1], hi - lo)
+
     me = lax.axis_index("tensor")
     valid_len = len_ref[0]
     barrier = pltpu.get_barrier_semaphore()
-    for k in range(1, tensors):
-        pl.semaphore_signal(barrier, inc=1, device_id={"tensor": lax.rem(me + k, tensors)}, device_id_type=MESH)
-    pl.semaphore_wait(barrier, tensors - 1)
+    if fast:
+        at = Place()
+        peers = [at.to_z(1), at.to_z(2), at.to_z(3), at.to_y, at.to_x, at.to_other, at.to_across]
+    else:
+        peers = [{"tensor": lax.rem(me + k, tensors)} for k in range(1, tensors)]
+    for peer in peers:
+        pl.semaphore_signal(barrier, inc=1, device_id=peer, device_id_type=MESH)
+    pl.semaphore_wait(barrier, len(peers))
+    if fast:
+        first = Gather(at, ref["part_a"], wa, ref["gather_send"].at[0], ref["gather_recv"].at[0])
+        second = Gather(at, ref["part_b"], wb, ref["gather_send"].at[1], ref["gather_recv"].at[1])
+        first.along_z()
+        first.own_on()
+        wa[at.c, at.a, at.b, at.z] = ref["part_a"][...]
+        wb[at.c, at.a, at.b, at.z] = ref["part_b"][...]
 
     lane = iota((64, 128), 1)
     low_lanes = lane < 64
@@ -194,19 +372,33 @@
     def joined(v):
         return jnp.where(low_lanes, v[:64], v[64:])
 
-    n1, r1 = normalised(x_ref[...].astype(F32))
+    x = x_ref[...].astype(F32)
+    cot = cot_ref[...].astype(F32)
+    if fast:
+        x, cot = mixed(x, True), mixed(cot, True)
+    ref["xs"][...] = x
+    ref["cots"][...] = cot
+    n1, r1 = normalised(x)
     n1s[...] = n1
     n1b = n1.astype(BF)
     valid = (iota((ROWS, 128), 0) + me * ROWS < valid_len).astype(F32)
+    rdiv[...] = row_divisors(me, tensors, valid_len)
+    for k in range(TILES):
+        wt[k] = tile_weights(k, me, tensors, valid_len)
+    if fast:
+        first.after_z()
+        second.along_z()
+        first.after_b()
+        first.after_a(0)
+        first.after_a(1)
+        second.own_on()
+        first.after_across()
     for t in range(PAIRS):
-        joint = nn(n1b[:, :256], wa_ref[t, 0]) + nn(n1b[:, 256:], wa_ref[t, 1])
+        joint = nn(n1b[:, :256], get(wa, t, 0, 0, 384)) + nn(n1b[:, 256:], get(wa, t, 1, 0, 384))
         joint = joint.astype(BF).astype(F32)
         qs[t, 0:ROWS, :] = joint[:, :128]
         ks[t, 0:ROWS, :] = joint[:, 128:256] * valid
         vs[t, 0:ROWS, :] = joint[:, 256:] * valid
-    rdiv[...] = row_divisors(me, tensors, valid_len)
-    for k in range(TILES):
-        wt[k] = tile_weights(k, me, tensors, valid_len)
 
     def pooling(p, carry):
         pool(qs.at[p])
@@ -288,6 +480,8 @@
 
     halos = (0, edge_l, halo_r, edge_r, halo_l, lambda k: far.at[me], lambda k: far.at[me])
     exchange(*halos)
+    if fast:
+        second.after_z()
     exchanged(*halos)
 
     def attend(p, carry):
@@ -329,43 +523,57 @@
         att[p] = num * inverse
         mm[p] = top
         dacc[p] = inverse
+        if fast:
+            pl.when(p == 0)(second.after_b)
+            pl.when(p == 1)(lambda: second.after_a(0))
+            pl.when(p == 3)(lambda: second.after_a(1))
         return carry
 
     lax.fori_loop(0, PAIRS, attend, 0)
 
+    if fast:
+        second.after_across()
     attb = [att[t].astype(BF) for t in range(PAIRS)]
     branch = []
     for y in range(2):
-        total = nt(attb[0], wb_ref[0, y, :, 0:128])
+        total = nt(attb[0], get(wb, 0, y, 0, 128))
         for t in range(1, PAIRS):
-            total = total + nt(attb[t], wb_ref[t, y, :, 0:128])
+            total = total + nt(attb[t], get(wb, t, y, 0, 128))
         branch.append(total)
     branch = jnp.concatenate(branch, axis=1)
-    middle = x_ref[...].astype(F32) + branch
+    middle = ref["xs"][...] + branch
     n2, r2 = normalised(middle)
     n2s[...] = n2
     n2b = n2.astype(BF)
     n2t = n2b.T
-    cotb = cot_ref[...]
+    cotb = ref["cots"][...].astype(BF)
     cott = cotb.T
 
+    if fast:
+        reduce_sems = lambda i: (ref["reduce_send"].at[i], ref["reduce_recv"].at[i])
+        late = Reduce(at, gb, ref["b0"], ref["b1"], ref["b2"], ref["b3"], *reduce_sems(1))
+        early = Reduce(at, ga, ref["a0"], ref["a1"], ref["a2"], ref["a3"], *reduce_sems(0))
+        late_parts = ((128, 1152, 0), (0, 128, 4))
+        early_parts = ((0, 384, 0),)
     dense, dn2 = [0.0, 0.0], [0.0, 0.0]
     for t in range(PAIRS):
-        pre = nn(n2b[:, :256], wb_ref[t, 0, :, 128:640]) + nn(n2b[:, 256:], wb_ref[t, 1, :, 128:640])
+        pre = nn(n2b[:, :256], get(wb, t, 0, 128, 640)) + nn(n2b[:, 256:], get(wb, t, 1, 128, 640))
         act, slope = gelu_both(pre)
         act = act.astype(BF)
-        act_grad = nn(cotb[:, :256], wb_ref[t, 0, :, 640:1152]) + nn(cotb[:, 256:], wb_ref[t, 1, :, 640:1152])
+        act_grad = nn(cotb[:, :256], get(wb, t, 0, 640, 1152)) + nn(cotb[:, 256:], get(wb, t, 1, 640, 1152))
         pre_grad = (act_grad * slope).astype(BF)
         for y in range(2):
             half = slice(256 * y, 256 * y + 256)
-            dense[y] = dense[y] + nt(act, wb_ref[t, y, :, 640:1152])
-            dn2[y] = dn2[y] + nt(pre_grad, wb_ref[t, y, :, 128:640])
-            gb_ref[t, y, :, 128:640] = nn(n2t[half, :], pre_grad).astype(BF)
-            gb_ref[t, y, :, 640:1152] = nn(cott[half, :], act).astype(BF)
+            dense[y] = dense[y] + nt(act, get(wb, t, y, 640, 1152))
+            dn2[y] = dn2[y] + nt(pre_grad, get(wb, t, y, 128, 640))
+            put(gb, t, y, 128, 640, nn(n2t[half, :], pre_grad))
+            put(gb, t, y, 640, 1152, nn(cott[half, :], act))
+        if fast:
+            late.across(t, 128, 1152, 0)
     dense = jnp.concatenate(dense, axis=1)
     dn2 = jnp.concatenate(dn2, axis=1)
     result = middle + dense
-    out_ref[...] = result.astype(BF)
+    out_ref[...] = (mixed(result, False) if fast else result).astype(BF)
     live = (iota((ROWS, 512), 0) + me * ROWS < valid_len).astype(F32)
     small_ref[2:3, :] = jnp.sum(live * result * result, axis=0, keepdims=True)
     small_ref[3:4, :] = jnp.sum(live * branch * branch, axis=0, keepdims=True)
@@ -374,14 +582,16 @@
     small_ref[6:8, :] = jnp.zeros((2, 512), F32)
     n2 = n2s[...]
     small_ref[1:2, :] = jnp.sum(dn2 * n2, axis=0, keepdims=True)
-    middle_grad = cotb.astype(F32) + norm_back(n2, r2, dn2)
+    middle_grad = ref["cots"][...] + norm_back(n2, r2, dn2)
     n2s[...] = middle_grad
     mgb = middle_grad.astype(BF)
     mgt = mgb.T
     for t in range(PAIRS):
-        us[t, 0:ROWS, :] = nn(mgb[:, :256], wb_ref[t, 0, :, 0:128]) + nn(mgb[:, 256:], wb_ref[t, 1, :, 0:128])
+        us[t, 0:ROWS, :] = nn(mgb[:, :256], get(wb, t, 0, 0, 128)) + nn(mgb[:, 256:], get(wb, t, 1, 0, 128))
         for y in range(2):
-            gb_ref[t, y, :, 0:128] = nn(mgt[256 * y : 256 * y + 256, :], att[t].astype(BF)).astype(BF)
+            put(gb, t, y, 0, 128, nn(mgt[256 * y : 256 * y + 256, :], att[t].astype(BF)))
+        if fast:
+            late.across(t, 0, 128, 4)
 
     def head_sums(v):
         first = jnp.sum(jnp.where(iota(v.shape, 1) < 64, v, 0.0), axis=-1, keepdims=True)
@@ -445,6 +655,9 @@
                 back_r[row, part, :] = dkw[row, RIGHT[level] : RIGHT[level] + 16, :].astype(BF)
             for g in range(tensors):
                 dfar[g, row] = dkw[row, FAR + 8 * g : FAR + 8 * g + 8, :]
+        if fast:
+            pl.when(p == 0)(lambda: late.far_half(late_parts))
+            pl.when(p == 2)(lambda: late.near_half(late_parts))
         return carry
 
     lax.fori_loop(0, PAIRS, attend_back, 0)
@@ -459,6 +672,8 @@
         lambda k: gfar.at[k],
     )
     exchange(*back)
+    if fast:
+        late.own_quarter(late_parts, ref["out_b"])
     exchanged(*back)
 
     def unpool(p, carry):
@@ -501,12 +716,45 @@
             [qs[t, 0:ROWS, :].astype(BF), ks[t, 0:ROWS, :].astype(BF), vs[t, 0:ROWS, :].astype(BF)], axis=1
         )
         for y in range(2):
-            ga_ref[t, y] = nn(n1t[256 * y : 256 * y + 256, :], joint).astype(BF)
-            dn1[y] = dn1[y] + nt(joint, wa_ref[t, y])
+            put(ga, t, y, 0, 384, nn(n1t[256 * y : 256 * y + 256, :], joint))
+            dn1[y] = dn1[y] + nt(joint, get(wa, t, y, 0, 384))
+        if fast:
+            early.across(t, 0, 384, 0)
     dn1 = jnp.concatenate(dn1, axis=1)
     small_ref[0:1, :] = jnp.sum(dn1 * n1, axis=0, keepdims=True)
-    r1 = lax.rsqrt(row_variance(x_ref[...].astype(F32)) + EPS)
-    ingrad_ref[...] = (n2s[...] + norm_back(n1, r1, dn1)).astype(BF)
+    if fast:
+        sums = Remote(ref["sum_send"], ref["sum_recv"])
+        got = ref["sums"]
+        for i, to in enumerate((at.to_other, at.to_x, at.to_y)):
+            if i == 1:
+                early.far_half(early_parts)
+            if i == 2:
+                early.near_half(early_parts)
+            got[2 * i] = small_ref[...]
+            sums.send(i, got.at[2 * i], got.at[2 * i + 1], to)
+            sums.arrived(i, got.at[2 * i + 1], to)
+            small_ref[...] = got[2 * i] + got[2 * i + 1]
+        got[6 + at.z] = small_ref[...]
+        for k in range(1, 4):
+            sums.send(2 + k, got.at[6 + at.z], got.at[6 + at.z], at.to_z(k))
+        early.own_quarter(early_parts, ref["out_a"])
+    r1 = lax.rsqrt(row_variance(ref["xs"][...]) + EPS)
+    in_grad = n2s[...] + norm_back(n1, r1, dn1)
+    ingrad_ref[...] = (mixed(in_grad, False) if fast else in_grad).astype(BF)
+    if fast:
+        late.finish(ref["out_b"])
+        early.finish(ref["out_a"])
+        for k in range(1, 4):
+            sums.arrived(2 + k, got.at[6], at.to_b)
+        small_ref[...] = ((got[6] + got[7]) + got[8]) + got[9]
+        late.across_drain(128, 1152, 0)
+        late.across_drain(0, 128, 4)
+        early.across_drain(0, 384, 0)
+        first.drain(ref["part_a"], at.to_x)
+        second.drain(ref["part_b"], at.to_x)
+        late.drain(late.r2.at[0], at.to_x)
+        early.drain(early.r2.at[0], at.to_x)
+        sums.drain(small_ref, at.to_x)
 
 
 def row_variance(v):
@@ -514,68 +762,93 @@
     return jnp.mean(centred * centred, axis=-1, keepdims=True)
 
 
-def run_layer(tensors, lengths, inputs, cotangent, wa, wb):
+def run_layer(fast, tensors, lengths, inputs, cotangent, wa, wb):
     vmem = pl.BlockSpec(memory_space=pltpu.VMEM)
     f = lambda *shape: pltpu.VMEM(shape, F32)
     b = lambda *shape: pltpu.VMEM(shape, BF)
+    full = (2, 2, 2, 4, 64) if fast else (tensors, 2, 256)
+    ca, cb = wa.shape[-1], wb.shape[-1]
+    outs = {"out": ((ROWS, 512), BF), "ingrad": ((ROWS, 512), BF), "small": ((8, 512), F32)}
+    scratch = {
+        "qs": f(PAIRS, STACK, 128),
+        "ks": f(PAIRS, STACK, 128),
+        "vs": f(PAIRS, STACK, 128),
+        "qb": b(PAIRS, STACK, 128),
+        "kw": b(PAIRS, KEYS, 128),
+        "vw": b(PAIRS, KEYS, 128),
+        "wt": f(TILES, 64, 128),
+        "rdiv": f(STACK, 128),
+        "edge_l": b(2 * PAIRS, HALO, 128),
+        "edge_r": b(2 * PAIRS, HALO, 128),
+        "halo_l": b(2 * PAIRS, HALO, 128),
+        "halo_r": b(2 * PAIRS, HALO, 128),
+        "far": f(tensors, 2 * PAIRS, 8, 128),
+        "eb": b(PAIRS, TILES, 128, 128),
+        "ns": f(STACK, 128),
+        "ml": f(PAIRS, STACK, 128),
+        "ds": f(STACK, 128),
+        "att": f(PAIRS, ROWS, 128),
+        "mm": f(PAIRS, ROWS, 128),
+        "tmp_a": f(ROWS, 128),
+        "tmp_b": f(ROWS, 128),
+        "tmp_c": f(ROWS, 128),
+        "xs": f(ROWS, 512),
+        "cots": f(ROWS, 512),
+        "n1s": f(ROWS, 512),
+        "n2s": f(ROWS, 512),
+        "dacc": f(PAIRS, ROWS, 128),
+        "us": f(PAIRS, STACK, 128),
+        "mus": f(STACK, 128),
+        "dqs": f(PAIRS, STACK, 128),
+        "dkw": f(2 * PAIRS, KEYS, 128),
+        "back_l": b(2 * PAIRS, HALO, 128),
+        "back_r": b(2 * PAIRS, HALO, 128),
+        "got_l": b(2 * PAIRS, HALO, 128),
+        "got_r": b(2 * PAIRS, HALO, 128),
+        "dfar": f(tensors, 2 * PAIRS, 8, 128),
+        "gfar": f(tensors, 2 * PAIRS, 8, 128),
+        "send_sem": pltpu.SemaphoreType.DMA((16,)),
+        "recv_sem": pltpu.SemaphoreType.DMA((16,)),
+    }
+    if fast:
+        ins = ("lengths", "x", "cot", "part_a", "part_b")
+        outs |= {"out_a": ((64, ca), F32), "out_b": ((64, cb), F32)}
+        for name, c in (("a", ca), ("b", cb)):
+            scratch |= {
+                "w" + name: b(*full, c),
+                "g" + name: b(*full, c),
+                name + "0": b(2, 2, 4, 64, c),
+                name + "1": b(2, 4, 64, c),
+                name + "2": b(4, 64, c),
+                name + "3": b(3, 64, c),
+            }
+        scratch |= {
+            "sums": f(10, 8, 512),
+            "gather_send": pltpu.SemaphoreType.DMA((2, 31)),
+            "gather_recv": pltpu.SemaphoreType.DMA((2, 31)),
+            "reduce_send": pltpu.SemaphoreType.DMA((2, 23)),
+            "reduce_recv": pltpu.SemaphoreType.DMA((2, 23)),
+            "sum_send": pltpu.SemaphoreType.DMA((6,)),
+            "sum_recv": pltpu.SemaphoreType.DMA((6,)),
+        }
+    else:
+        ins = ("lengths", "x", "cot", "wa", "wb")
+        outs |= {"ga": (wa.shape, BF), "gb": (wb.shape, BF)}
     return pl.pallas_call(
-        functools.partial(layer_kernel, tensors),
-        out_shape=(
-            jax.ShapeDtypeStruct((ROWS, 512), BF),
-            jax.ShapeDtypeStruct((ROWS, 512), BF),
-            jax.ShapeDtypeStruct(wa.shape, BF),
-            jax.ShapeDtypeStruct(wb.shape, BF),
-            jax.ShapeDtypeStruct((8, 512), F32),
-        ),
-        in_specs=[pl.BlockSpec(memory_space=pltpu.SMEM), vmem, vmem, vmem, vmem],
+        functools.partial(layer_kernel, fast, tensors, (*ins, *outs, *scratch)),
+        out_shape=tuple(jax.ShapeDtypeStruct(*shape) for shape in outs.values()),
+        in_specs=[pl.BlockSpec(memory_space=pltpu.SMEM)] + [vmem] * 4,
         out_specs=(vmem,) * 5,
-        scratch_shapes=[
-            f(PAIRS, STACK, 128),
-            f(PAIRS, STACK, 128),
-            f(PAIRS, STACK, 128),
-            b(PAIRS, STACK, 128),
-            b(PAIRS, KEYS, 128),
-            b(PAIRS, KEYS, 128),
-            f(TILES, 64, 128),
-            f(STACK, 128),
-            b(2 * PAIRS, HALO, 128),
-            b(2 * PAIRS, HALO, 128),
-            b(2 * PAIRS, HALO, 128),
-            b(2 * PAIRS, HALO, 128),
-            f(tensors, 2 * PAIRS, 8, 128),
-            b(PAIRS, TILES, 128, 128),
-            f(STACK, 128),
-            f(PAIRS, STACK, 128),
-            f(STACK, 128),
-            f(PAIRS, ROWS, 128),
-            f(PAIRS, ROWS, 128),
-            f(ROWS, 128),
-            f(ROWS, 128),
-            f(ROWS, 128),
-            f(ROWS, 512),
-            f(ROWS, 512),
-            f(PAIRS, ROWS, 128),
-            f(PAIRS, STACK, 128),
-            f(STACK, 128),
-            f(PAIRS, STACK, 128),
-            f(2 * PAIRS, KEYS, 128),
-            b(2 * PAIRS, HALO, 128),
-            b(2 * PAIRS, HALO, 128),
-            b(2 * PAIRS, HALO, 128),
-            b(2 * PAIRS, HALO, 128),
-            f(tensors, 2 * PAIRS, 8, 128),
-            f(tensors, 2 * PAIRS, 8, 128),
-            pltpu.SemaphoreType.DMA((16,)),
-            pltpu.SemaphoreType.DMA((16,)),
-        ],
+        scratch_shapes=list(scratch.values()),
         compiler_params=pltpu.CompilerParams(
-            collective_id=0, has_side_effects=True, vmem_limit_bytes=60 * 1024 * 1024
+            collective_id=0, has_side_effects=True, vmem_limit_bytes=62 * 1024 * 1024
         ),
         name="layer",
     )(lengths, inputs, cotangent, wa, wb)
 
 
 def per_device(
+    fast,
     inputs,
     lengths,
     cotangent,
@@ -595,18 +868,22 @@
     scaled = lambda g, w: (g * w.astype(F32)).astype(BF)
     part_a = scaled(g1, jnp.concatenate([query_weight, key_weight, value_weight], axis=1))
     part_b = jnp.concatenate([output_weight.T, scaled(g2, inner_weight), outer_weight.T], axis=1)
-    wa = lax.all_gather(part_a, everyone, axis=0, tiled=True).reshape(tensors, 2, 256, 384)
-    wb = lax.all_gather(part_b, everyone, axis=0, tiled=True).reshape(tensors, 2, 256, 1152)
-    out, input_grad, ga, gb, small = run_layer(tensors, lengths, inputs, cotangent, wa, wb)
-    width = first_gain.shape[0]
-
-    def reduced(g):
-        return lax.psum_scatter(
-            g.reshape(tensors * 512, g.shape[-1]).astype(F32), everyone, scatter_dimension=0, tiled=True
-        )
-
-    ga, gb, small = reduced(ga), reduced(gb), lax.psum(small, everyone)
-    at = lax.axis_index("dp") * width
+    width, group = first_gain.shape[0], lax.axis_index("dp")
+    if fast:
+        out, input_grad, small, ga, gb = run_layer(fast, tensors, lengths, inputs, cotangent, part_a, part_b)
+        at = (group % 2) * 256 + (group // 2) * 64
+    else:
+        wa = lax.all_gather(part_a, everyone, axis=0, tiled=True).reshape(tensors, 2, 256, 384)
+        wb = lax.all_gather(part_b, everyone, axis=0, tiled=True).reshape(tensors, 2, 256, 1152)
+        out, input_grad, small, ga, gb = run_layer(fast, tensors, lengths, inputs, cotangent, wa, wb)
+
+        def reduced(g):
+            return lax.psum_scatter(
+                g.reshape(tensors * 512, g.shape[-1]).astype(F32), everyone, scatter_dimension=0, tiled=True
+            )
+
+        ga, gb, small = reduced(ga), reduced(gb), lax.psum(small, everyone)
+        at = group * width
     gains = lax.dynamic_slice(small, (0, at), (2, width))
     sums = jnp.sum(small, axis=1)
     root_mean_squares = jnp.sqrt(sums[2:5] / sums[5])
@@ -627,8 +904,9 @@
 
 
 def solution(mesh):
+    fast = (mesh.shape["dp"], mesh.shape["tensor"]) == (8, 4)
     return jax.shard_map(
-        per_device,
+        functools.partial(per_device, fast),
         mesh=mesh,
         in_specs=(
             P(("dp", "tensor"), None),

time: 431 us -> 117 us (0.27)
  waiting for transfers between devices: 313 us -> 0 us
  Pallas kernels: 38.6 us -> 101 us
  blocking collectives: 40.4 us -> 0 us
  other arithmetic: 19.6 us -> 5.8 us
  between operations: 14.5 us -> 1.5 us
    reduce_scatter x2 -> x0, waiting for transfers between devices: 191 us -> none  [reduced(): lax.psum_scatter(g.reshape(tensors * 512, g.shape[-1]).astype(F32), every...]
    all_gather x2 -> x0, waiting for transfers between devices: 122 us -> none  [the longest x1 65.9 us: per_device(): lax.all_gather(part_b, everyone, axis=0, tiled=True)]
    pallas_call x1, Pallas kernels: 38.6 us -> 101 us  [run_layer(): pl.pallas_call(functools.partial(layer_kernel, fast, tensors, (*ins, *out...]
    psum x1 -> x0, blocking collectives: 40.4 us -> none  [per_device(): ga, gb, small = (reduced(ga), reduced(gb), lax.psum(small, everyone))]
    convert_element_type x2 -> x0, other arithmetic: 9.81 us -> none  [reduced(): g.reshape(tensors * 512, g.shape[-1]).astype(F32)]
  transfers between devices with their start and end apart: 4 -> 0, of which waited for: 4 -> 0; matrix products, arithmetic and copies ran while one was open for 3% -> 0% of each run, Pallas kernels for 0% -> 0%
where the time goes in v2:
time: 117 us; the launch traced here: 114 us
  Pallas kernels  101 us (86%)
  other arithmetic  5.8 us (5%)
  local copies, waits for them, and re-layouts  5.59 us (5%)
  between operations  1.5 us (1%)
    pallas_call x1, Pallas kernels, run_layer(): pl.pallas_call(functools.partial(layer_kernel, fast, tensors, (*ins, *out...  101 us
    unnamed x24, local copies, waits for them, and re-layouts  2.84 us

profile of v2, /device:TPU:0, one launch (start us, length us, event | category | flops | bytes accessed | tf_op | source)
XLA Modules:
  0.0 114.4 jit_solution(7587220389574968540)
XLA Ops:
  0.7 0.0 copy-start.8
  0.7 0.0 copy-start.9
  0.7 0.0 copy-start.10
  0.7 0.0 copy-start.6
  0.7 0.0 copy-start.7
  0.7 0.0 copy-start.3
  1.4 0.0 copy-done.9
  1.4 0.0 copy-done.10
  1.5 0.0 copy-done.8
  1.5 0.0 copy-done.6
  1.5 0.0 copy-done.7
  1.5 0.7 multiply_convert_fusion.1.refs_3_
  2.2 0.0 copy-done.3
  2.2 0.1 multiply_convert_fusion
  2.3 0.8 copy-done.4
  3.0 0.0 copy-done.5
  3.0 0.7 pad_maximum_fusion.refs_4_
  3.7 101.5 %layer.1 = (bf16[256,512]{1,0:T(8,128)(2,1)}, bf16[256,512]{1,0:T(8,128)(2,1)}, f32[8,512]{1,0:T(8,128)}, f32[64,384]{1,0:T(8,128)}, f32[64,1152]{1,0:T(8,128)}) custom-call(s32[1]{0:T(128)S(6)} %copy.24.refs_0_, bf16[256,512]{1,0:T(8,128)(2,1)} %refs_1_.1, bf16[256,512]{1,0:T(8,128)(2,1)} %refs_2_.1, bf16[64,384]{1,0:T(8,128)(2,1)} %multiply_convert_fusion.1.refs_3_, ...), custom_call_target="tpu_custom_call" | custom-call | tf_op jit(solution)/shard_map/layer/pallas_call | solution.py:837
  105.2 0.0 copy-start
  105.2 0.9 reduce_sum.9
  106.1 0.6 slice.39
  106.7 0.8 constant_dynamic-slice_fusion
  107.4 1.2 %divide_sqrt_fusion = f32[3]{0:T(128)} fusion(f32[8]{0:T(128)S(1)} %reduce_sum.9, f32[]{:T(128)} %bitcast.6), kind=kLoop, calls=%fused_computation.9 | loop fusion | flops 3 | bytes 28 | tf_op jit(solution)/shard_map/sqrt | solution.py:889
  108.7 0.5 bitcast_divide_fusion
  109.2 1.0 broadcast_multiply_fusion
  110.2 1.4 %fusion = (f32[64,128]{1,0:T(8,128)}, f32[64,128]{1,0:T(8,128)}, f32[64,128]{1,0:T(8,128)}, f32[128,64]{0,1:T(8,128)}) fusion(f32[64,384]{1,0:T(8,128)S(1)} %broadcast_multiply_fusion, f32[64,1152]{1,0:T(8,128)} %get-tuple-element.19), kind=kLoop, calls=%fused_computation.11 | loop fusion | bytes 262144 | tf_op jit(solution)/shard_map/slice | solution.py:896
  111.6 0.0 copy-done
  111.6 0.7 slice_bitcast_fusion
  112.3 0.3 copy-done.2
  112.6 0.7 copy.25
  113.3 0.3 copy-done.1
  113.7 0.7 copy.26
  (6 shorter events, 0.0 us)
Async XLA Ops:
  0.7 0.8 copy-start.8
  0.7 0.8 copy-start.9
  0.7 0.8 copy-start.10
  0.7 0.8 copy-start.6
  0.7 0.8 copy-start.7
  0.7 1.5 %copy-start.3 = (bf16[64,512]{1,0:T(8,128)(2,1)S(1)}, bf16[64,512]{1,0:T(8,128)(2,1)}, u32[]{:S(2)}) copy-start(bf16[64,512]{1,0:T(8,128)(2,1)} %param.18) | copy-start | bytes 196612
  2.2 0.8 copy-start.4
  2.2 0.8 copy-start.5
  105.2 6.4 %copy-start = (f32[64,1152]{1,0:T(8,128)S(1)}, f32[64,1152]{1,0:T(8,128)}, u32[]{:S(2)}) copy-start(f32[64,1152]{1,0:T(8,128)} %get-tuple-element.19) | copy-start | bytes 884740
  111.6 1.0 copy-start.2
  112.6 1.0 copy-start.1

commit v3 on v2

--- a/solution.py
+++ b/solution.py
@@ -200,21 +200,21 @@
         self.along_a(0, 0)
         self.across(0, 0, 0)
 
-    def after_z(self):
-        for j in (1, 3, 2):
+    def after_z(self, *js):
+        for j in js:
             self.arrived(j - 1, self.shard(j), self.at.to_b)
             self.along_b(j)
             self.along_a(j, 0)
             self.across(j, 0, 0)
 
-    def after_b(self):
-        for j in (0, 1, 3, 2):
+    def after_b(self, *js):
+        for j in js:
             self.arrived(3 + j, self.shard(j, 0, 1), self.at.to_b)
             self.along_a(j, 1)
             self.across(j, 0, 1)
 
-    def after_a(self, bb):
-        for j in (0, 1, 3, 2):
+    def after_a(self, bb, *js):
+        for j in js:
             self.arrived(7 + 4 * bb + j, self.shard(j, 1, bb), self.at.to_b)
             self.across(j, 1, bb)
 
@@ -251,24 +251,26 @@
             piece = self.r0.at[i // 2, i % 2, :, :, lo:hi]
             self.copy(base + i, piece, piece, self.at.to_other).wait_send()
 
-    def far_half(self, parts):
+    def across_all(self, parts):
+        for a in range(2):
+            for b in range(2):
+                for lo, hi, base in parts:
+                    self.across_wait(a, b, lo, hi, base)
+
+    def far(self, *js):
         at = self.at
-        for bb in (1, 0):
-            b = flipped(at.b, bb)
-            for lo, hi, base in parts:
-                self.across_wait(1 - at.a, b, lo, hi, base)
-            for j in range(4):
-                z = (at.z + j) % 4
+        for j in js:
+            z = (at.z + j) % 4
+            for bb in (1, 0):
+                b = flipped(at.b, bb)
                 here = self.g.at[at.c, 1 - at.a, b, z]
                 here[...] = (here[...].astype(F32) + self.r0[1 - at.a, b, z].astype(F32)).astype(BF)
                 self.send(8 + 4 * bb + j, here, self.r1.at[b, z], at.to_a)
 
-    def near_half(self, parts):
+    def near(self, *js):
         at = self.at
         b = 1 - at.b
-        for lo, hi, base in parts:
-            self.across_wait(at.a, b, lo, hi, base)
-        for j in range(4):
+        for j in js:
             z = (at.z + j) % 4
             here = self.g.at[at.c, at.a, b, z]
             self.arrived(12 + j, self.r1.at[b, z], at.to_a)
@@ -276,12 +278,10 @@
             here[...] = total.astype(BF)
             self.send(16 + j, here, self.r2.at[z], at.to_b)
 
-    def own_quarter(self, parts, out):
+    def own(self, out, *js):
         at = self.at
         b = at.b
-        for lo, hi, base in parts:
-            self.across_wait(at.a, b, lo, hi, base)
-        for j in (1, 3, 2, 0):
+        for j in js:
             z = (at.z + j) % 4
             here = self.g.at[at.c, at.a, b, z]
             self.arrived(8 + j, self.r1.at[b, z], at.to_a)
@@ -327,8 +327,8 @@
         ref[n] for n in ("back_l", "back_r", "got_l", "got_r", "dfar", "gfar")
     )
     send_sem, recv_sem, small_ref = ref["send_sem"], ref["recv_sem"], ref["small"]
-    ga, gb = ref["ga"], ref["gb"]
-    wa, wb = (ref["wa"], ref["wb"])
+    ga, gm, gl = ref["ga"], ref["gm"], ref["gl"]
+    wa, wm, wl = ref["wa"], ref["wm"], ref["wl"]
 
     def view(r, t, y):
         if not fast:
@@ -354,12 +354,26 @@
         pl.semaphore_signal(barrier, inc=1, device_id=peer, device_id_type=MESH)
     pl.semaphore_wait(barrier, len(peers))
     if fast:
-        first = Gather(at, ref["part_a"], wa, ref["gather_send"].at[0], ref["gather_recv"].at[0])
-        second = Gather(at, ref["part_b"], wb, ref["gather_send"].at[1], ref["gather_recv"].at[1])
+        first, second, third = (
+            Gather(at, ref["part_" + n], ref["w" + n], ref["gather_send"].at[i], ref["gather_recv"].at[i])
+            for i, n in enumerate("aml")
+        )
+        early, middle_sum, late = (
+            Reduce(
+                at,
+                ref["g" + n],
+                *(ref[n + str(k)] for k in range(4)),
+                ref["reduce_send"].at[i],
+                ref["reduce_recv"].at[i],
+            )
+            for i, n in enumerate("aml")
+        )
+        early_parts, middle_parts, late_parts = ((0, 384, 0),), ((128, 640, 0), (0, 128, 4)), ((0, 512, 0),)
         first.along_z()
         first.own_on()
-        wa[at.c, at.a, at.b, at.z] = ref["part_a"][...]
-        wb[at.c, at.a, at.b, at.z] = ref["part_b"][...]
+        second.own_on()
+        for n in "aml":
+            ref["w" + n][at.c, at.a, at.b, at.z] = ref["part_" + n][...]
 
     lane = iota((64, 128), 1)
     low_lanes = lane < 64
@@ -386,12 +400,14 @@
     for k in range(TILES):
         wt[k] = tile_weights(k, me, tensors, valid_len)
     if fast:
-        first.after_z()
+        first.after_z(1, 3, 2)
         second.along_z()
-        first.after_b()
-        first.after_a(0)
-        first.after_a(1)
-        second.own_on()
+        first.after_b(0, 1, 3, 2)
+        second.after_b(0)
+        first.after_a(0, 0, 1, 3, 2)
+        first.after_a(1, 0, 1, 3, 2)
+        second.after_a(0, 0)
+        third.own_on()
         first.after_across()
     for t in range(PAIRS):
         joint = nn(n1b[:, :256], get(wa, t, 0, 0, 384)) + nn(n1b[:, 256:], get(wa, t, 1, 0, 384))
@@ -407,7 +423,6 @@
         for which, (raw, windows) in enumerate(((ks, kw), (vs, vw))):
             raw_p = raw.at[p]
             pool(raw_p)
-            row = which * PAIRS + p
             for start, n in BLANK:
                 windows[p, start : start + n, :] = jnp.zeros((n, 128), BF)
             for level in range(LEVELS - 1):
@@ -416,13 +431,12 @@
                 coarse = (raw_p[rows, :] * rdiv[rows, :]).astype(BF)
                 if level < 4:
                     windows[p, OWN[level] : OWN[level] + n, :] = coarse
-                edge_l[row, 16 * level : 16 * level + 16, :] = coarse[:16]
-                edge_r[row, 16 * level : 16 * level + 16, :] = coarse[n - 16 :]
+                edge_l[p, which, 16 * level : 16 * level + 16, :] = coarse[:16]
+                edge_r[p, which, 16 * level : 16 * level + 16, :] = coarse[n - 16 :]
             rows = slice(AT[5], AT[5] + 8)
-            far[me, row] = raw_p[rows, :] * rdiv[rows, :]
+            far[me, p, which] = raw_p[rows, :] * rdiv[rows, :]
+        exchange(*halos(p))
         return carry
-
-    lax.fori_loop(0, PAIRS, pooling, 0)
 
     def to_left(src, dst, sem):
         return pltpu.make_async_remote_copy(
@@ -478,19 +492,22 @@
         for k in range(1, tensors):
             to_peer(k, far_src(k), far_dst(k), base + 1 + k).wait()
 
-    halos = (0, edge_l, halo_r, edge_r, halo_l, lambda k: far.at[me], lambda k: far.at[me])
-    exchange(*halos)
-    if fast:
-        second.after_z()
-    exchanged(*halos)
+    def halos(p):
+        block = lambda k: far.at[me, p]
+        return (5 * p, edge_l.at[p], halo_r.at[p], edge_r.at[p], halo_l.at[p], block, block)
+
+    lax.fori_loop(0, PAIRS, pooling, 0)
+    if fast:
+        second.after_z(1, 3)
+        third.along_z()
 
     def attend(p, carry):
+        exchanged(*halos(p))
         for which, windows in enumerate((kw, vw)):
-            row = which * PAIRS + p
             for level in range(LEVELS - 1):
-                windows[p, LEFT[level] : LEFT[level] + 16, :] = halo_l[row, 16 * level : 16 * level + 16, :]
-                windows[p, RIGHT[level] : RIGHT[level] + 16, :] = halo_r[row, 16 * level : 16 * level + 16, :]
-            groups = jnp.concatenate([far[g, row] for g in range(tensors)], axis=0)
+                windows[p, LEFT[level] : LEFT[level] + 16, :] = halo_l[p, which, 16 * level : 16 * level + 16, :]
+                windows[p, RIGHT[level] : RIGHT[level] + 16, :] = halo_r[p, which, 16 * level : 16 * level + 16, :]
+            groups = jnp.concatenate([far[g, p, which] for g in range(tensors)], axis=0)
             windows[p, FAR:KEYS, :] = groups.astype(BF)
         for k in range(TILES):
             here = slice(64 * k, 64 * k + 64)
@@ -507,6 +524,27 @@
             ns[here, :] = joined(nn(low, vw[p, keys, :]))
             ml[p, here, :] = joined(jnp.broadcast_to(m, (128, 128)))
             ds_[here, :] = joined(jnp.broadcast_to(total, (128, 128)))
+            if fast and k == 3:
+
+                @pl.when(p == 1)
+                def _():
+                    second.after_b(3)
+                    second.after_a(0, 1)
+
+                @pl.when(p == 2)
+                def _():
+                    second.after_a(1, 1)
+                    second.after_a(0, 2)
+                    third.after_z(1)
+                    third.after_a(0, 0)
+
+                @pl.when(p == 3)
+                def _():
+                    second.after_a(1, 2)
+                    third.after_z(2)
+                    third.after_b(1)
+                    third.after_a(1, 0)
+
         rows = slice(AT[5], AT[5] + 8)
         num, top, den = ns[rows, :], ml[p, rows, :], ds_[rows, :]
         for level in range(LEVELS - 2, -1, -1):
@@ -524,9 +562,29 @@
         mm[p] = top
         dacc[p] = inverse
         if fast:
-            pl.when(p == 0)(second.after_b)
-            pl.when(p == 1)(lambda: second.after_a(0))
-            pl.when(p == 3)(lambda: second.after_a(1))
+
+            @pl.when(p == 0)
+            def _():
+                second.after_z(2)
+                second.after_b(1)
+                second.after_a(1, 0)
+
+            @pl.when(p == 1)
+            def _():
+                second.after_b(2)
+                second.after_a(0, 3)
+                third.after_b(0)
+
+            @pl.when(p == 2)
+            def _():
+                second.after_a(1, 3)
+                third.after_z(3)
+
+            @pl.when(p == 3)
+            def _():
+                third.after_a(0, 1)
+                third.after_b(3)
+
         return carry
 
     lax.fori_loop(0, PAIRS, attend, 0)
@@ -536,9 +594,9 @@
     attb = [att[t].astype(BF) for t in range(PAIRS)]
     branch = []
     for y in range(2):
-        total = nt(attb[0], get(wb, 0, y, 0, 128))
+        total = nt(attb[0], get(wm, 0, y, 0, 128))
         for t in range(1, PAIRS):
-            total = total + nt(attb[t], get(wb, t, y, 0, 128))
+            total = total + nt(attb[t], get(wm, t, y, 0, 128))
         branch.append(total)
     branch = jnp.concatenate(branch, axis=1)
     middle = ref["xs"][...] + branch
@@ -546,30 +604,45 @@
     n2s[...] = n2
     n2b = n2.astype(BF)
     n2t = n2b.T
+    if fast:
+        third.after_b(2)
+        third.after_a(0, 3)
+        third.after_a(1, 1)
     cotb = ref["cots"][...].astype(BF)
     cott = cotb.T
 
-    if fast:
-        reduce_sems = lambda i: (ref["reduce_send"].at[i], ref["reduce_recv"].at[i])
-        late = Reduce(at, gb, ref["b0"], ref["b1"], ref["b2"], ref["b3"], *reduce_sems(1))
-        early = Reduce(at, ga, ref["a0"], ref["a1"], ref["a2"], ref["a3"], *reduce_sems(0))
-        late_parts = ((128, 1152, 0), (0, 128, 4))
-        early_parts = ((0, 384, 0),)
+    acts, slopes = ref["acts"], ref["slopes"]
+    for t in range(PAIRS):
+        pre = nn(n2b[:, :256], get(wm, t, 0, 128, 640)) + nn(n2b[:, 256:], get(wm, t, 1, 128, 640))
+        act, slope = gelu_both(pre)
+        act = act.astype(BF)
+        acts[t] = act
+        slopes[t] = slope
+        for y in range(2):
+            put(gl, t, y, 0, 512, nn(cott[256 * y : 256 * y + 256, :], act))
+        if fast:
+            late.across(t, 0, 512, 0)
+            if t == 1:
+                third.after_a(0, 2)
+            if t == 2:
+                third.after_a(1, 3)
+    if fast:
+        third.after_a(1, 2)
+        third.after_across()
+        late.across_all(late_parts)
     dense, dn2 = [0.0, 0.0], [0.0, 0.0]
     for t in range(PAIRS):
-        pre = nn(n2b[:, :256], get(wb, t, 0, 128, 640)) + nn(n2b[:, 256:], get(wb, t, 1, 128, 640))
-        act, slope = gelu_both(pre)
-        act = act.astype(BF)
-        act_grad = nn(cotb[:, :256], get(wb, t, 0, 640, 1152)) + nn(cotb[:, 256:], get(wb, t, 1, 640, 1152))
-        pre_grad = (act_grad * slope).astype(BF)
+        if fast:
+            late.far((1, 3, 2, 0)[t])
+        act_grad = nn(cotb[:, :256], get(wl, t, 0, 0, 512)) + nn(cotb[:, 256:], get(wl, t, 1, 0, 512))
+        pre_grad = (act_grad * slopes[t]).astype(BF)
+        act = acts[t]
         for y in range(2):
-            half = slice(256 * y, 256 * y + 256)
-            dense[y] = dense[y] + nt(act, get(wb, t, y, 640, 1152))
-            dn2[y] = dn2[y] + nt(pre_grad, get(wb, t, y, 128, 640))
-            put(gb, t, y, 128, 640, nn(n2t[half, :], pre_grad))
-            put(gb, t, y, 640, 1152, nn(cott[half, :], act))
+            dense[y] = dense[y] + nt(act, get(wl, t, y, 0, 512))
+            dn2[y] = dn2[y] + nt(pre_grad, get(wm, t, y, 128, 640))
+            put(gm, t, y, 128, 640, nn(n2t[256 * y : 256 * y + 256, :], pre_grad))
         if fast:
-            late.across(t, 128, 1152, 0)
+            middle_sum.across(t, 128, 640, 0)
     dense = jnp.concatenate(dense, axis=1)
     dn2 = jnp.concatenate(dn2, axis=1)
     result = middle + dense
@@ -587,11 +660,13 @@
     mgb = middle_grad.astype(BF)
     mgt = mgb.T
     for t in range(PAIRS):
-        us[t, 0:ROWS, :] = nn(mgb[:, :256], get(wb, t, 0, 0, 128)) + nn(mgb[:, 256:], get(wb, t, 1, 0, 128))
+        us[t, 0:ROWS, :] = nn(mgb[:, :256], get(wm, t, 0, 0, 128)) + nn(mgb[:, 256:], get(wm, t, 1, 0, 128))
         for y in range(2):
-            put(gb, t, y, 0, 128, nn(mgt[256 * y : 256 * y + 256, :], att[t].astype(BF)))
+            put(gm, t, y, 0, 128, nn(mgt[256 * y : 256 * y + 256, :], att[t].astype(BF)))
         if fast:
-            late.across(t, 0, 128, 4)
+            middle_sum.across(t, 0, 128, 4)
+    if fast:
+        late.near(1, 3)
 
     def head_sums(v):
         first = jnp.sum(jnp.where(iota(v.shape, 1) < 64, v, 0.0), axis=-1, keepdims=True)
@@ -647,36 +722,72 @@
                 dkw[p, keys, :] = dk
                 dkw[PAIRS + p, keys, :] = dv
             dqs[p, here, :] = joined(nn(d, kw[p, keys, :]))
+            if fast and k == 3:
+
+                @pl.when(p == 0)
+                def _():
+                    late.near(2)
+
+                @pl.when(p == 1)
+                def _():
+                    late.own(ref["out_l"], 1)
+                    middle_sum.far(3)
+
+                @pl.when(p == 2)
+                def _():
+                    middle_sum.far(2)
+                    late.own(ref["out_l"], 2)
+
+                @pl.when(p == 3)
+                def _():
+                    late.own(ref["out_l"], 0)
+                    middle_sum.far(0)
+
         for which in range(2):
             row = which * PAIRS + p
             for level in range(LEVELS - 1):
                 part = slice(16 * level, 16 * level + 16)
-                back_l[row, part, :] = dkw[row, LEFT[level] : LEFT[level] + 16, :].astype(BF)
-                back_r[row, part, :] = dkw[row, RIGHT[level] : RIGHT[level] + 16, :].astype(BF)
+                back_l[p, which, part, :] = dkw[row, LEFT[level] : LEFT[level] + 16, :].astype(BF)
+                back_r[p, which, part, :] = dkw[row, RIGHT[level] : RIGHT[level] + 16, :].astype(BF)
             for g in range(tensors):
-                dfar[g, row] = dkw[row, FAR + 8 * g : FAR + 8 * g + 8, :]
+                dfar[g, p, which] = dkw[row, FAR + 8 * g : FAR + 8 * g + 8, :]
+        exchange(*back(p))
         if fast:
-            pl.when(p == 0)(lambda: late.far_half(late_parts))
-            pl.when(p == 2)(lambda: late.near_half(late_parts))
+
+            @pl.when(p == 0)
+            def _():
+                middle_sum.across_all(middle_parts)
+                middle_sum.far(1)
+                late.near(0)
+
+            @pl.when(p == 1)
+            def _():
+                late.own(ref["out_l"], 3)
+
+            @pl.when(p == 2)
+            def _():
+                middle_sum.near(1)
+
+            @pl.when(p == 3)
+            def _():
+                middle_sum.near(3)
+
         return carry
 
+    def back(p):
+        return (
+            20 + 5 * p,
+            back_l.at[p],
+            got_r.at[p],
+            back_r.at[p],
+            got_l.at[p],
+            lambda k: dfar.at[lax.rem(me + k, tensors), p],
+            lambda k: gfar.at[k, p],
+        )
+
     lax.fori_loop(0, PAIRS, attend_back, 0)
-
-    back = (
-        8,
-        back_l,
-        got_r,
-        back_r,
-        got_l,
-        lambda k: dfar.at[lax.rem(me + k, tensors)],
-        lambda k: gfar.at[k],
-    )
-    exchange(*back)
-    if fast:
-        late.own_quarter(late_parts, ref["out_b"])
-    exchanged(*back)
-
     def unpool(p, carry):
+        exchanged(*back(p))
         factors = stack_factors()
         cur = dqs[p, AT[5] : AT[5] + 8, :] * factors[AT[5] : AT[5] + 8]
         for level in range(LEVELS - 2, -1, -1):
@@ -686,9 +797,9 @@
         for which, raw in enumerate((ks, vs)):
             row = which * PAIRS + p
             raw_p = raw.at[p]
-            cur = gfar[1, row]
+            cur = gfar[1, p, which]
             for k in range(2, tensors):
-                cur = cur + gfar[k, row]
+                cur = cur + gfar[k, p, which]
             cur = cur * rdiv[AT[5] : AT[5] + 8, :]
             for level in range(LEVELS - 2, -1, -1):
                 n = COUNT[level]
@@ -700,13 +811,15 @@
                     raw_p[rows, :] = jnp.zeros((n, 128), F32)
                 first = slice(AT[level], AT[level] + 16)
                 last = slice(AT[level] + n - 16, AT[level] + n)
-                raw_p[first, :] = raw_p[first, :] + got_l[row, part, :].astype(F32)
-                raw_p[last, :] = raw_p[last, :] + got_r[row, part, :].astype(F32)
+                raw_p[first, :] = raw_p[first, :] + got_l[p, which, part, :].astype(F32)
+                raw_p[last, :] = raw_p[last, :] + got_r[p, which, part, :].astype(F32)
                 cur = doubled(tmp_a, cur, n // 2) + raw_p[rows, :] * rdiv[rows, :]
             raw_p[0:ROWS, :] = cur * (iota((ROWS, 128), 0) + me * ROWS < valid_len).astype(F32)
         return carry
 
     lax.fori_loop(0, PAIRS, unpool, 0)
+    if fast:
+        middle_sum.own(ref["out_m"], 1)
 
     n1 = n1s[...]
     n1t = n1.astype(BF).T
@@ -725,35 +838,50 @@
     if fast:
         sums = Remote(ref["sum_send"], ref["sum_recv"])
         got = ref["sums"]
-        for i, to in enumerate((at.to_other, at.to_x, at.to_y)):
-            if i == 1:
-                early.far_half(early_parts)
-            if i == 2:
-                early.near_half(early_parts)
+        ways = (at.to_other, at.to_x, at.to_y)
+
+        def sum_send(i):
             got[2 * i] = small_ref[...]
-            sums.send(i, got.at[2 * i], got.at[2 * i + 1], to)
-            sums.arrived(i, got.at[2 * i + 1], to)
+            sums.send(i, got.at[2 * i], got.at[2 * i + 1], ways[i])
+
+        def sum_add(i):
+            sums.arrived(i, got.at[2 * i + 1], ways[i])
             small_ref[...] = got[2 * i] + got[2 * i + 1]
+
+        sum_send(0)
+        middle_sum.near(2)
+        early.across_all(early_parts)
+        early.far(1, 3, 2, 0)
+        sum_add(0)
+        sum_send(1)
+        middle_sum.own(ref["out_m"], 3)
+        middle_sum.near(0)
+        sum_add(1)
+        sum_send(2)
+        middle_sum.own(ref["out_m"], 2)
+        early.near(1, 3, 2, 0)
+        sum_add(2)
         got[6 + at.z] = small_ref[...]
         for k in range(1, 4):
             sums.send(2 + k, got.at[6 + at.z], got.at[6 + at.z], at.to_z(k))
-        early.own_quarter(early_parts, ref["out_a"])
+        middle_sum.own(ref["out_m"], 0)
+        early.own(ref["out_a"], 1, 3, 2, 0)
     r1 = lax.rsqrt(row_variance(ref["xs"][...]) + EPS)
     in_grad = n2s[...] + norm_back(n1, r1, dn1)
     ingrad_ref[...] = (mixed(in_grad, False) if fast else in_grad).astype(BF)
     if fast:
-        late.finish(ref["out_b"])
+        late.finish(ref["out_l"])
+        middle_sum.finish(ref["out_m"])
         early.finish(ref["out_a"])
         for k in range(1, 4):
             sums.arrived(2 + k, got.at[6], at.to_b)
         small_ref[...] = ((got[6] + got[7]) + got[8]) + got[9]
-        late.across_drain(128, 1152, 0)
-        late.across_drain(0, 128, 4)
-        early.across_drain(0, 384, 0)
-        first.drain(ref["part_a"], at.to_x)
-        second.drain(ref["part_b"], at.to_x)
-        late.drain(late.r2.at[0], at.to_x)
-        early.drain(early.r2.at[0], at.to_x)
+        for remote, parts in ((early, early_parts), (middle_sum, middle_parts), (late, late_parts)):
+            for lo, hi, base in parts:
+                remote.across_drain(lo, hi, base)
+            remote.drain(remote.r2.at[0], at.to_x)
+        for remote in (first, second, third):
+            remote.drain(remote.own, at.to_x)
         sums.drain(small_ref, at.to_x)
 
 
@@ -762,12 +890,12 @@
     return jnp.mean(centred * centred, axis=-1, keepdims=True)
 
 
-def run_layer(fast, tensors, lengths, inputs, cotangent, wa, wb):
+def run_layer(fast, tensors, lengths, inputs, cotangent, *weights):
     vmem = pl.BlockSpec(memory_space=pltpu.VMEM)
     f = lambda *shape: pltpu.VMEM(shape, F32)
     b = lambda *shape: pltpu.VMEM(shape, BF)
     full = (2, 2, 2, 4, 64) if fast else (tensors, 2, 256)
-    ca, cb = wa.shape[-1], wb.shape[-1]
+    groups = dict(zip("aml", weights, strict=True))
     outs = {"out": ((ROWS, 512), BF), "ingrad": ((ROWS, 512), BF), "small": ((8, 512), F32)}
     scratch = {
         "qs": f(PAIRS, STACK, 128),
@@ -778,11 +906,11 @@
         "vw": b(PAIRS, KEYS, 128),
         "wt": f(TILES, 64, 128),
         "rdiv": f(STACK, 128),
-        "edge_l": b(2 * PAIRS, HALO, 128),
-        "edge_r": b(2 * PAIRS, HALO, 128),
-        "halo_l": b(2 * PAIRS, HALO, 128),
-        "halo_r": b(2 * PAIRS, HALO, 128),
-        "far": f(tensors, 2 * PAIRS, 8, 128),
+        "edge_l": b(PAIRS, 2, HALO, 128),
+        "edge_r": b(PAIRS, 2, HALO, 128),
+        "halo_l": b(PAIRS, 2, HALO, 128),
+        "halo_r": b(PAIRS, 2, HALO, 128),
+        "far": f(tensors, PAIRS, 2, 8, 128),
         "eb": b(PAIRS, TILES, 128, 128),
         "ns": f(STACK, 128),
         "ml": f(PAIRS, STACK, 128),
@@ -800,20 +928,23 @@
         "us": f(PAIRS, STACK, 128),
         "mus": f(STACK, 128),
         "dqs": f(PAIRS, STACK, 128),
+        "acts": b(PAIRS, ROWS, 512),
+        "slopes": f(PAIRS, ROWS, 512),
         "dkw": f(2 * PAIRS, KEYS, 128),
-        "back_l": b(2 * PAIRS, HALO, 128),
-        "back_r": b(2 * PAIRS, HALO, 128),
-        "got_l": b(2 * PAIRS, HALO, 128),
-        "got_r": b(2 * PAIRS, HALO, 128),
-        "dfar": f(tensors, 2 * PAIRS, 8, 128),
-        "gfar": f(tensors, 2 * PAIRS, 8, 128),
-        "send_sem": pltpu.SemaphoreType.DMA((16,)),
-        "recv_sem": pltpu.SemaphoreType.DMA((16,)),
+        "back_l": b(PAIRS, 2, HALO, 128),
+        "back_r": b(PAIRS, 2, HALO, 128),
+        "got_l": b(PAIRS, 2, HALO, 128),
+        "got_r": b(PAIRS, 2, HALO, 128),
+        "dfar": f(tensors, PAIRS, 2, 8, 128),
+        "gfar": f(tensors, PAIRS, 2, 8, 128),
+        "send_sem": pltpu.SemaphoreType.DMA((40,)),
+        "recv_sem": pltpu.SemaphoreType.DMA((40,)),
     }
     if fast:
-        ins = ("lengths", "x", "cot", "part_a", "part_b")
-        outs |= {"out_a": ((64, ca), F32), "out_b": ((64, cb), F32)}
-        for name, c in (("a", ca), ("b", cb)):
+        ins = ("lengths", "x", "cot", "part_a", "part_m", "part_l")
+        for name, part in groups.items():
+            c = part.shape[-1]
+            outs |= {"out_" + name: ((64, c), F32)}
             scratch |= {
                 "w" + name: b(*full, c),
                 "g" + name: b(*full, c),
@@ -824,27 +955,27 @@
             }
         scratch |= {
             "sums": f(10, 8, 512),
-            "gather_send": pltpu.SemaphoreType.DMA((2, 31)),
-            "gather_recv": pltpu.SemaphoreType.DMA((2, 31)),
-            "reduce_send": pltpu.SemaphoreType.DMA((2, 23)),
-            "reduce_recv": pltpu.SemaphoreType.DMA((2, 23)),
+            "gather_send": pltpu.SemaphoreType.DMA((3, 31)),
+            "gather_recv": pltpu.SemaphoreType.DMA((3, 31)),
+            "reduce_send": pltpu.SemaphoreType.DMA((3, 23)),
+            "reduce_recv": pltpu.SemaphoreType.DMA((3, 23)),
             "sum_send": pltpu.SemaphoreType.DMA((6,)),
             "sum_recv": pltpu.SemaphoreType.DMA((6,)),
         }
     else:
-        ins = ("lengths", "x", "cot", "wa", "wb")
-        outs |= {"ga": (wa.shape, BF), "gb": (wb.shape, BF)}
+        ins = ("lengths", "x", "cot", "wa", "wm", "wl")
+        outs |= {"g" + name: (w.shape, BF) for name, w in groups.items()}
     return pl.pallas_call(
         functools.partial(layer_kernel, fast, tensors, (*ins, *outs, *scratch)),
         out_shape=tuple(jax.ShapeDtypeStruct(*shape) for shape in outs.values()),
-        in_specs=[pl.BlockSpec(memory_space=pltpu.SMEM)] + [vmem] * 4,
-        out_specs=(vmem,) * 5,
+        in_specs=[pl.BlockSpec(memory_space=pltpu.SMEM)] + [vmem] * 5,
+        out_specs=(vmem,) * 6,
         scratch_shapes=list(scratch.values()),
         compiler_params=pltpu.CompilerParams(
             collective_id=0, has_side_effects=True, vmem_limit_bytes=62 * 1024 * 1024
         ),
         name="layer",
-    )(lengths, inputs, cotangent, wa, wb)
+    )(lengths, inputs, cotangent, *weights)
 
 
 def per_device(
@@ -867,22 +998,23 @@
     g2 = second_gain.astype(F32)[:, None]
     scaled = lambda g, w: (g * w.astype(F32)).astype(BF)
     part_a = scaled(g1, jnp.concatenate([query_weight, key_weight, value_weight], axis=1))
-    part_b = jnp.concatenate([output_weight.T, scaled(g2, inner_weight), outer_weight.T], axis=1)
+    part_m = jnp.concatenate([output_weight.T, scaled(g2, inner_weight)], axis=1)
+    parts = (part_a, part_m, outer_weight.T)
     width, group = first_gain.shape[0], lax.axis_index("dp")
     if fast:
-        out, input_grad, small, ga, gb = run_layer(fast, tensors, lengths, inputs, cotangent, part_a, part_b)
+        out, input_grad, small, ga, gm, gl = run_layer(fast, tensors, lengths, inputs, cotangent, *parts)
         at = (group % 2) * 256 + (group // 2) * 64
     else:
-        wa = lax.all_gather(part_a, everyone, axis=0, tiled=True).reshape(tensors, 2, 256, 384)
-        wb = lax.all_gather(part_b, everyone, axis=0, tiled=True).reshape(tensors, 2, 256, 1152)
-        out, input_grad, small, ga, gb = run_layer(fast, tensors, lengths, inputs, cotangent, wa, wb)
+        full = [lax.all_gather(p, everyone, axis=0, tiled=True).reshape(tensors, 2, 256, -1) for p in parts]
+        out, input_grad, small, *grads = run_layer(fast, tensors, lengths, inputs, cotangent, *full)
 
         def reduced(g):
             return lax.psum_scatter(
                 g.reshape(tensors * 512, g.shape[-1]).astype(F32), everyone, scatter_dimension=0, tiled=True
             )
 
-        ga, gb, small = reduced(ga), reduced(gb), lax.psum(small, everyone)
+        ga, gm, gl = (reduced(g) for g in grads)
+        small = lax.psum(small, everyone)
         at = group * width
     gains = lax.dynamic_slice(small, (0, at), (2, width))
     sums = jnp.sum(small, axis=1)
@@ -894,9 +1026,9 @@
         ga[:, 0:128],
         ga[:, 128:256],
         ga[:, 256:384],
-        gb[:, 0:128].T,
-        gb[:, 128:640] * g2,
-        gb[:, 640:1152].T,
+        gm[:, 0:128].T,
+        gm[:, 128:640] * g2,
+        gl.T,
         gains[0] / first_gain.astype(F32),
         gains[1] / second_gain.astype(F32),
         root_mean_squares,

time: 117 us -> 107 us (0.915); the launches traced: 114 us -> 107 us
  Pallas kernels: 101 us -> 94.1 us
    pallas_call x1, Pallas kernels: 101 us -> 94.1 us  [run_layer(): pl.pallas_call(functools.partial(layer_kernel, fast, tensors, (*ins, *out...]
    unnamed x24 -> x25, local copies, waits for them, and re-layouts: 2.84 us -> 3.45 us
where the time goes in v3:
time: 107 us
  Pallas kernels  94.1 us (88%)
  other arithmetic  5.87 us (5%)
  local copies, waits for them, and re-layouts  5.47 us (5%)
  between operations  1.42 us (1%)
    pallas_call x1, Pallas kernels, run_layer(): pl.pallas_call(functools.partial(layer_kernel, fast, tensors, (*ins, *out...  94.1 us
    unnamed x25, local copies, waits for them, and re-layouts  3.45 us

profile of v3, /device:TPU:0, one launch (start us, length us, event | category | flops | bytes accessed | tf_op | source)
XLA Modules:
  0.0 106.8 jit_solution(13733162337199208950)
XLA Ops:
  0.7 0.0 copy-start.10
  0.7 0.6 copy-done.10
  1.3 0.9 multiply_convert_fusion
  2.3 0.0 copy-done.5
  2.3 0.0 copy-start.9
  2.3 0.0 copy-start.6
  2.3 0.0 copy-start.7
  2.3 0.0 copy-start.8
  2.3 0.6 pad_maximum_fusion.refs_4_
  3.0 0.0 copy-done.9
  3.0 0.0 copy-done.6
  3.0 0.0 copy-done.7
  3.0 0.0 copy-done.8
  3.0 0.7 multiply_convert_fusion.1.refs_3_
  4.4 94.1 %layer.1 = (bf16[256,512]{1,0:T(8,128)(2,1)}, bf16[256,512]{1,0:T(8,128)(2,1)}, f32[8,512]{1,0:T(8,128)}, f32[64,384]{1,0:T(8,128)}, f32[64,640]{1,0:T(8,128)}, /*index=5*/f32[64,512]{1,0:T(8,128)}) custom-call(s32[1]{0:T(128)S(6)} %copy.25.refs_0_, bf16[256,512]{1,0:T(8,128)(2,1)} %refs_1_.1, bf16[256,512]{1,0:T(8,128)(2,1)} %refs_2_.1, ...), custom_call_target="tpu_custom_call" | custom-call | tf_op jit(solution)/shard_map/layer/pallas_call | solution.py:968
  98.5 0.0 copy-start.2
  98.5 0.8 constant_dynamic-slice_fusion
  99.3 0.5 bitcast_divide_fusion
  99.8 1.0 broadcast_multiply_fusion
  100.8 0.0 copy-done.2
  100.8 0.0 copy-start.1
  100.8 0.7 fusion
  101.5 0.0 copy-done.4
  101.5 0.1 reduce_sum.9
  101.6 0.6 slice.35
  102.2 1.2 %divide_sqrt_fusion = f32[3]{0:T(128)} fusion(f32[8]{0:T(128)S(1)} %reduce_sum.9, f32[]{:T(128)} %bitcast.6), kind=kLoop, calls=%fused_computation.8 | loop fusion | flops 3 | bytes 28 | tf_op jit(solution)/shard_map/sqrt | solution.py:1021
  103.4 0.7 slice_multiply_fusion
  104.1 0.7 copy.26
  104.9 0.3 copy-done
  105.2 0.7 copy.27
  105.9 0.3 copy-done.3
  106.2 0.7 copy.28
  (7 shorter events, 0.0 us)
Async XLA Ops:
  0.7 0.7 copy-start.10
  1.3 0.9 copy-start.5
  2.3 0.7 copy-start.9
  2.3 0.7 copy-start.6
  2.3 0.7 copy-start.7
  2.3 0.7 copy-start.8
  98.5 2.3 %copy-start.2 = (f32[64,640]{1,0:T(8,128)S(1)}, f32[64,640]{1,0:T(8,128)}, u32[]{:S(2)}) copy-start(f32[64,640]{1,0:T(8,128)} %get-tuple-element.20) | copy-start | bytes 491524
  99.8 1.7 %copy-start.4 = (f32[8,512]{1,0:T(8,128)S(1)}, f32[8,512]{1,0:T(8,128)}, u32[]{:S(2)}) copy-start(f32[8,512]{1,0:T(8,128)} %get-tuple-element.22) | copy-start | bytes 49156
  100.8 3.3 %copy-start.1 = (bf16[256,512]{1,0:T(8,128)(2,1)S(1)}, bf16[256,512]{1,0:T(8,128)(2,1)}, u32[]{:S(2)}) copy-start(bf16[256,512]{1,0:T(8,128)(2,1)} %get-tuple-element.40) | copy-start | bytes 786436
  104.1 1.0 copy-start
  105.2 1.0 copy-start.3

commit v4 on v3

--- a/solution.py
+++ b/solution.py
@@ -25,6 +25,18 @@
 TILE_AT = (0, 64, 128, 192, 320, 384, 512, 640)
 TILES = 8
 HALO = 80
+LOADS = (
+    ("g1", (64,)),
+    ("g2", (64,)),
+    ("q", (64, 128)),
+    ("k", (64, 128)),
+    ("v", (64, 128)),
+    ("o", (64, 128)),
+    ("w1", (64, 512)),
+    ("part_l", (64, 512)),
+    ("x", (ROWS, 512)),
+    ("cot", (ROWS, 512)),
+)
 
 
 def nn(a, b):
@@ -317,7 +329,37 @@
 
 def layer_kernel(fast, tensors, names, *refs):
     ref = dict(zip(names, refs, strict=True))
-    len_ref, x_ref, cot_ref, out_ref, ingrad_ref = (ref[n] for n in ("lengths", "x", "cot", "out", "ingrad"))
+    if fast:
+        loads = {
+            n: pltpu.make_async_copy(ref["in_" + n], ref[n], ref["in_sem"].at[i]) for i, (n, _) in enumerate(LOADS)
+        }
+        for load in loads.values():
+            load.start()
+    me = lax.axis_index("tensor")
+    valid_len = ref["lengths"][0]
+    barrier = pltpu.get_barrier_semaphore()
+    if fast:
+        at = Place()
+        peers = [at.to_z(1), at.to_z(2), at.to_z(3), at.to_y, at.to_x, at.to_other, at.to_across]
+    else:
+        peers = [{"tensor": lax.rem(me + k, tensors)} for k in range(1, tensors)]
+    for peer in peers:
+        pl.semaphore_signal(barrier, inc=1, device_id=peer, device_id_type=MESH)
+    len_ref, x_ref, cot_ref = (ref[n] for n in ("lengths", "x", "cot"))
+    if fast:
+        out_ref, ingrad_ref = ref["rows"].at[:, 0:512], ref["rows"].at[:, 512:1024]
+        outs = {"a": ref["grads"].at[:, 0:384], "m": ref["grads"].at[:, 384:1024], "l": ref["grads"].at[:, 1024:1536]}
+        for n, _ in LOADS[:8]:
+            loads[n].wait()
+        g1, g2 = (ref[n][...].astype(F32).reshape(1, 64) for n in ("g1", "g2"))
+        column = lambda g: jnp.sum(jnp.where(iota((64, 64), 0) == iota((64, 64), 1), g, 0.0), axis=1, keepdims=True)
+        g1c, g2c = column(g1), column(g2)
+        for i, n in enumerate("qkv"):
+            ref["part_a"][:, 128 * i : 128 * i + 128] = (g1c * ref[n][...].astype(F32)).astype(BF)
+        ref["part_m"][:, 0:128] = ref["o"][...]
+        ref["part_m"][:, 128:640] = (g2c * ref["w1"][...].astype(F32)).astype(BF)
+    else:
+        out_ref, ingrad_ref = ref["out"], ref["ingrad"]
     qs, ks, vs, qb, kw, vw, wt, rdiv = (ref[n] for n in ("qs", "ks", "vs", "qb", "kw", "vw", "wt", "rdiv"))
     edge_l, edge_r, halo_l, halo_r, far = (ref[n] for n in ("edge_l", "edge_r", "halo_l", "halo_r", "far"))
     eb, ns, ml, ds_, att, mm = (ref[n] for n in ("eb", "ns", "ml", "ds", "att", "mm"))
@@ -342,16 +384,6 @@
         v = view(r, t, y)
         v[..., lo:hi] = value.astype(BF).reshape(*v.shape[:-1], hi - lo)
 
-    me = lax.axis_index("tensor")
-    valid_len = len_ref[0]
-    barrier = pltpu.get_barrier_semaphore()
-    if fast:
-        at = Place()
-        peers = [at.to_z(1), at.to_z(2), at.to_z(3), at.to_y, at.to_x, at.to_other, at.to_across]
-    else:
-        peers = [{"tensor": lax.rem(me + k, tensors)} for k in range(1, tensors)]
-    for peer in peers:
-        pl.semaphore_signal(barrier, inc=1, device_id=peer, device_id_type=MESH)
     pl.semaphore_wait(barrier, len(peers))
     if fast:
         first, second, third = (
@@ -386,6 +418,9 @@
     def joined(v):
         return jnp.where(low_lanes, v[:64], v[64:])
 
+    if fast:
+        loads["x"].wait()
+        loads["cot"].wait()
     x = x_ref[...].astype(F32)
     cot = cot_ref[...].astype(F32)
     if fast:
@@ -730,17 +765,17 @@
 
                 @pl.when(p == 1)
                 def _():
-                    late.own(ref["out_l"], 1)
+                    late.own(outs["l"], 1)
                     middle_sum.far(3)
 
                 @pl.when(p == 2)
                 def _():
                     middle_sum.far(2)
-                    late.own(ref["out_l"], 2)
+                    late.own(outs["l"], 2)
 
                 @pl.when(p == 3)
                 def _():
-                    late.own(ref["out_l"], 0)
+                    late.own(outs["l"], 0)
                     middle_sum.far(0)
 
         for which in range(2):
@@ -762,7 +797,7 @@
 
             @pl.when(p == 1)
             def _():
-                late.own(ref["out_l"], 3)
+                late.own(outs["l"], 3)
 
             @pl.when(p == 2)
             def _():
@@ -819,7 +854,7 @@
 
     lax.fori_loop(0, PAIRS, unpool, 0)
     if fast:
-        middle_sum.own(ref["out_m"], 1)
+        middle_sum.own(outs["m"], 1)
 
     n1 = n1s[...]
     n1t = n1.astype(BF).T
@@ -854,28 +889,41 @@
         early.far(1, 3, 2, 0)
         sum_add(0)
         sum_send(1)
-        middle_sum.own(ref["out_m"], 3)
+        middle_sum.own(outs["m"], 3)
         middle_sum.near(0)
         sum_add(1)
         sum_send(2)
-        middle_sum.own(ref["out_m"], 2)
+        middle_sum.own(outs["m"], 2)
         early.near(1, 3, 2, 0)
         sum_add(2)
         got[6 + at.z] = small_ref[...]
         for k in range(1, 4):
             sums.send(2 + k, got.at[6 + at.z], got.at[6 + at.z], at.to_z(k))
-        middle_sum.own(ref["out_m"], 0)
-        early.own(ref["out_a"], 1, 3, 2, 0)
+        middle_sum.own(outs["m"], 0)
+        early.own(outs["a"], 1, 3, 2, 0)
     r1 = lax.rsqrt(row_variance(ref["xs"][...]) + EPS)
     in_grad = n2s[...] + norm_back(n1, r1, dn1)
     ingrad_ref[...] = (mixed(in_grad, False) if fast else in_grad).astype(BF)
     if fast:
-        late.finish(ref["out_l"])
-        middle_sum.finish(ref["out_m"])
-        early.finish(ref["out_a"])
+        late.finish(outs["l"])
+        middle_sum.finish(outs["m"])
+        outs["m"][:, 128:640] = outs["m"][:, 128:640] * g2c
+        early.finish(outs["a"])
+        outs["a"][...] = outs["a"][...] * g1c
         for k in range(1, 4):
             sums.arrived(2 + k, got.at[6], at.to_b)
-        small_ref[...] = ((got[6] + got[7]) + got[8]) + got[9]
+        total = ((got[6] + got[7]) + got[8]) + got[9]
+        gains = jnp.zeros((2, 64), F32)
+        for i in range(8):
+            gains = gains + jnp.where(4 * at.y + at.z == i, total[0:2, 64 * i : 64 * i + 64], 0.0)
+        squares = jnp.sum(total[2:6], axis=1, keepdims=True)
+        root = jnp.sqrt(squares[0:3] / squares[3:4])
+        lanes = iota((1, 128), 1)
+        tail = ref["grads"].at[:, 1536:1664]
+        tail[...] = jnp.zeros(tail.shape, F32)
+        tail[0:1, 0:64] = gains[0:1] / g1
+        tail[1:2, 0:64] = gains[1:2] / g2
+        tail[2:3, :] = sum(jnp.where(lanes == i, root[i : i + 1], 0.0) for i in range(3))
         for remote, parts in ((early, early_parts), (middle_sum, middle_parts), (late, late_parts)):
             for lo, hi, base in parts:
                 remote.across_drain(lo, hi, base)
@@ -895,8 +943,6 @@
     f = lambda *shape: pltpu.VMEM(shape, F32)
     b = lambda *shape: pltpu.VMEM(shape, BF)
     full = (2, 2, 2, 4, 64) if fast else (tensors, 2, 256)
-    groups = dict(zip("aml", weights, strict=True))
-    outs = {"out": ((ROWS, 512), BF), "ingrad": ((ROWS, 512), BF), "small": ((8, 512), F32)}
     scratch = {
         "qs": f(PAIRS, STACK, 128),
         "ks": f(PAIRS, STACK, 128),
@@ -941,10 +987,12 @@
         "recv_sem": pltpu.SemaphoreType.DMA((40,)),
     }
     if fast:
-        ins = ("lengths", "x", "cot", "part_a", "part_m", "part_l")
-        for name, part in groups.items():
-            c = part.shape[-1]
-            outs |= {"out_" + name: ((64, c), F32)}
+        ins = ("lengths", *("in_" + n for n in ("x", "cot", "q", "k", "v", "o", "w1", "part_l", "g1", "g2")))
+        outs = {"rows": ((ROWS, 1024), BF), "grads": ((64, 1664), F32)}
+        scratch |= {n: b(*shape) for n, shape in LOADS}
+        scratch |= {"in_sem": pltpu.SemaphoreType.DMA((len(LOADS),))}
+        scratch |= {"part_a": b(64, 384), "part_m": b(64, 640), "small": f(8, 512)}
+        for name, c in zip("aml", (384, 640, 512), strict=True):
             scratch |= {
                 "w" + name: b(*full, c),
                 "g" + name: b(*full, c),
@@ -964,18 +1012,47 @@
         }
     else:
         ins = ("lengths", "x", "cot", "wa", "wm", "wl")
-        outs |= {"g" + name: (w.shape, BF) for name, w in groups.items()}
+        outs = {"out": ((ROWS, 512), BF), "ingrad": ((ROWS, 512), BF), "small": ((8, 512), F32)}
+        outs |= {"g" + name: (w.shape, BF) for name, w in zip("aml", weights, strict=True)}
     return pl.pallas_call(
         functools.partial(layer_kernel, fast, tensors, (*ins, *outs, *scratch)),
         out_shape=tuple(jax.ShapeDtypeStruct(*shape) for shape in outs.values()),
-        in_specs=[pl.BlockSpec(memory_space=pltpu.SMEM)] + [vmem] * 5,
-        out_specs=(vmem,) * 6,
+        in_specs=[pl.BlockSpec(memory_space=pltpu.SMEM)] + [pl.BlockSpec(memory_space=pltpu.HBM) if fast else vmem] * (len(ins) - 1),
+        out_specs=(vmem,) * len(outs),
         scratch_shapes=list(scratch.values()),
         compiler_params=pltpu.CompilerParams(
             collective_id=0, has_side_effects=True, vmem_limit_bytes=62 * 1024 * 1024
         ),
         name="layer",
     )(lengths, inputs, cotangent, *weights)
+
+
+def hand_out_kernel(rows, grads, *refs):
+    outs, tail, sem = refs[:11], refs[11], refs[12]
+    edges = (0, 128, 256, 384, 512, 1024, 1536)
+    parts = [rows.at[:, 0:512], rows.at[:, 512:1024]]
+    parts += [grads.at[:, lo:hi] for lo, hi in zip(edges, edges[1:])]
+    copies = [pltpu.make_async_copy(grads.at[0:8, 1536:1664], tail, sem.at[8])]
+    copies += [pltpu.make_async_copy(part, out, sem.at[i]) for i, (part, out) in enumerate(zip(parts, outs))]
+    for copy in copies:
+        copy.start()
+    copies[0].wait()
+    for i in range(3):
+        outs[8 + i][...] = tail[i, 0 : outs[8 + i].shape[0]]
+    for copy in copies[1:]:
+        copy.wait()
+
+
+def hand_out(rows, grads):
+    shapes = [(ROWS, 512)] * 2 + [(64, 128)] * 4 + [(64, 512)] * 2 + [(64,)] * 2 + [(3,)]
+    return pl.pallas_call(
+        hand_out_kernel,
+        out_shape=tuple(jax.ShapeDtypeStruct(shape, BF if i < 2 else F32) for i, shape in enumerate(shapes)),
+        in_specs=[pl.BlockSpec(memory_space=pltpu.HBM)] * 2,
+        out_specs=tuple(pl.BlockSpec(memory_space=pltpu.VMEM) for _ in shapes),
+        scratch_shapes=[pltpu.VMEM((8, 128), F32), pltpu.SemaphoreType.DMA((9,))],
+        name="hand_out",
+    )(rows, grads)
 
 
 def per_device(
@@ -992,31 +1069,44 @@
     first_gain,
     second_gain,
 ):
-    tensors, groups = lax.axis_size("tensor"), lax.axis_size("dp")
+    tensors = lax.axis_size("tensor")
     everyone = ("tensor", "dp")
+    if fast:
+        rows, grads = run_layer(
+            fast,
+            tensors,
+            lengths,
+            inputs,
+            cotangent,
+            query_weight,
+            key_weight,
+            value_weight,
+            output_weight.T,
+            inner_weight,
+            outer_weight.T,
+            first_gain,
+            second_gain,
+        )
+        out, input_grad, gq, gk, gv, go, gi, gl, gain_one, gain_two, root = hand_out(rows, grads)
+        return out, input_grad, gq, gk, gv, go.T, gi, gl.T, gain_one, gain_two, root
     g1 = first_gain.astype(F32)[:, None]
     g2 = second_gain.astype(F32)[:, None]
     scaled = lambda g, w: (g * w.astype(F32)).astype(BF)
     part_a = scaled(g1, jnp.concatenate([query_weight, key_weight, value_weight], axis=1))
     part_m = jnp.concatenate([output_weight.T, scaled(g2, inner_weight)], axis=1)
     parts = (part_a, part_m, outer_weight.T)
-    width, group = first_gain.shape[0], lax.axis_index("dp")
-    if fast:
-        out, input_grad, small, ga, gm, gl = run_layer(fast, tensors, lengths, inputs, cotangent, *parts)
-        at = (group % 2) * 256 + (group // 2) * 64
-    else:
-        full = [lax.all_gather(p, everyone, axis=0, tiled=True).reshape(tensors, 2, 256, -1) for p in parts]
-        out, input_grad, small, *grads = run_layer(fast, tensors, lengths, inputs, cotangent, *full)
-
-        def reduced(g):
-            return lax.psum_scatter(
-                g.reshape(tensors * 512, g.shape[-1]).astype(F32), everyone, scatter_dimension=0, tiled=True
-            )
-
-        ga, gm, gl = (reduced(g) for g in grads)
-        small = lax.psum(small, everyone)
-        at = group * width
-    gains = lax.dynamic_slice(small, (0, at), (2, width))
+    full = [lax.all_gather(p, everyone, axis=0, tiled=True).reshape(tensors, 2, 256, -1) for p in parts]
+    out, input_grad, small, *grads = run_layer(fast, tensors, lengths, inputs, cotangent, *full)
+
+    def reduced(g):
+        return lax.psum_scatter(
+            g.reshape(tensors * 512, g.shape[-1]).astype(F32), everyone, scatter_dimension=0, tiled=True
+        )
+
+    ga, gm, gl = (reduced(g) for g in grads)
+    small = lax.psum(small, everyone)
+    width = first_gain.shape[0]
+    gains = lax.dynamic_slice(small, (0, lax.axis_index("dp") * width), (2, width))
     sums = jnp.sum(small, axis=1)
     root_mean_squares = jnp.sqrt(sums[2:5] / sums[5])
     ga = ga * g1

time: 107 us -> 97 us (0.907)
  other arithmetic: 5.87 us -> 0 us
  local copies, waits for them, and re-layouts: 5.47 us -> 0 us
  Pallas kernels: 94.1 us -> 95.3 us
    unnamed x25 -> x0, local copies, waits for them, and re-layouts: 3.45 us -> none
    pallas_call x0 -> x1, Pallas kernels: none -> 2.18 us  [hand_out(): pl.pallas_call(hand_out_kernel, out_shape=tuple((jax.ShapeDtypeStruct(sha...]
    mul x2 -> x0, other arithmetic: 1.71 us -> none  [the longest x1 0.98 us: per_device(): ga = ga * g1]
    convert_element_type x4 -> x0, other arithmetic: 1.63 us -> none  [the longest x2 1.63 us: per_device(): scaled = lambda g, w: (g * w.astype(F32)).astype(BF)]
    slice x2 -> x0, local copies, waits for them, and re-layouts: 1.24 us -> none  [the longest x1 0.65 us: per_device(): ga[:, 256:384]]
    sqrt x1 -> x0, other arithmetic: 1.23 us -> none  [per_device(): root_mean_squares = jnp.sqrt(sums[2:5] / sums[5])]
where the time goes in v4:
time: 97 us; the launch traced here: 96.7 us
  Pallas kernels  95.3 us (98%)
  between operations  1.46 us (2%)
    pallas_call x1, Pallas kernels, run_layer(): pl.pallas_call(functools.partial(layer_kernel, fast, tensors, (*ins, *out...  93.1 us
    pallas_call x1, Pallas kernels, hand_out(): pl.pallas_call(hand_out_kernel, out_shape=tuple((jax.ShapeDtypeStruct(sha...  2.18 us

profile of v4, /device:TPU:0, one launch (start us, length us, event | category | flops | bytes accessed | tf_op | source)
XLA Modules:
  0.0 96.7 jit_solution(7191766082499190248)
XLA Ops:
  1.3 93.1 %layer.1 = (bf16[256,1024]{1,0:T(8,128)(2,1)}, f32[64,1664]{1,0:T(8,128)}) custom-call(s32[1]{0:T(128)S(6)} %copy.22.refs_0_, bf16[256,512]{1,0:T(8,128)(2,1)} %refs_1_.1, bf16[256,512]{1,0:T(8,128)(2,1)} %refs_2_.1, bf16[64,128]{1,0:T(8,128)(2,1)} %refs_3_.1, bf16[64,128]{1,0:T(8,128)(2,1)} %refs_4_.1, bf16[64,128]{1,0:T(8,128)(2,1)} %refs_5_.1, ...), custom_call_target="tpu_custom_call" | custom-call | tf_op jit(solution)/shard_map/layer/pallas_call | solution.py:1017
  94.4 2.2 %hand_out.1 = (bf16[256,512]{1,0:T(8,128)(2,1)}, bf16[256,512]{1,0:T(8,128)(2,1)}, f32[64,128]{1,0:T(8,128)}, f32[64,128]{1,0:T(8,128)}, f32[64,128]{1,0:T(8,128...) custom-call(bf16[256,1024]{1,0:T(8,128)(2,1)} %get-tuple-element.24., ...), custom_call_target="tpu_custom_call" | custom-call | tf_op jit(solution)/shard_map/hand_out/pallas_call | solution.py:1048

commit v5 on v4

--- a/solution.py
+++ b/solution.py
@@ -207,23 +207,26 @@
     def across(self, j, aa, bb):
         self.send(15 + 8 * aa + 4 * bb + j, self.source(j, aa, bb), self.shard(j, aa, bb), self.at.to_other)
 
-    def own_on(self):
+    def own_on(self, met=True):
         self.along_b(0)
         self.along_a(0, 0)
-        self.across(0, 0, 0)
-
-    def after_z(self, *js):
+        if met:
+            self.across(0, 0, 0)
+
+    def after_z(self, *js, met=True):
         for j in js:
             self.arrived(j - 1, self.shard(j), self.at.to_b)
             self.along_b(j)
             self.along_a(j, 0)
-            self.across(j, 0, 0)
-
-    def after_b(self, *js):
+            if met:
+                self.across(j, 0, 0)
+
+    def after_b(self, *js, met=True):
         for j in js:
             self.arrived(3 + j, self.shard(j, 0, 1), self.at.to_b)
             self.along_a(j, 1)
-            self.across(j, 0, 1)
+            if met:
+                self.across(j, 0, 1)
 
     def after_a(self, bb, *js):
         for j in js:
@@ -340,11 +343,19 @@
     barrier = pltpu.get_barrier_semaphore()
     if fast:
         at = Place()
-        peers = [at.to_z(1), at.to_z(2), at.to_z(3), at.to_y, at.to_x, at.to_other, at.to_across]
+        same = [at.to_z(1), at.to_z(2), at.to_z(3), at.to_y, at.to_x]
+        others = [at.to_other, at.to_across]
+        for peer in same:
+            pl.semaphore_signal(barrier, inc=1, device_id=peer, device_id_type=MESH)
+
+        @pl.when(at.c == 0)
+        def _():
+            for peer in others:
+                pl.semaphore_signal(barrier, inc=1, device_id=peer, device_id_type=MESH)
     else:
         peers = [{"tensor": lax.rem(me + k, tensors)} for k in range(1, tensors)]
-    for peer in peers:
-        pl.semaphore_signal(barrier, inc=1, device_id=peer, device_id_type=MESH)
+        for peer in peers:
+            pl.semaphore_signal(barrier, inc=1, device_id=peer, device_id_type=MESH)
     len_ref, x_ref, cot_ref = (ref[n] for n in ("lengths", "x", "cot"))
     if fast:
         out_ref, ingrad_ref = ref["rows"].at[:, 0:512], ref["rows"].at[:, 512:1024]
@@ -384,8 +395,17 @@
         v = view(r, t, y)
         v[..., lo:hi] = value.astype(BF).reshape(*v.shape[:-1], hi - lo)
 
-    pl.semaphore_wait(barrier, len(peers))
-    if fast:
+    if fast:
+        @pl.when(at.c == 0)
+        def _():
+            pl.semaphore_wait(barrier, len(same))
+
+        @pl.when(at.c == 1)
+        def _():
+            pl.semaphore_wait(barrier, len(same) + len(others))
+            for peer in others:
+                pl.semaphore_signal(ref["ready"], inc=1, device_id=peer, device_id_type=MESH)
+
         first, second, third = (
             Gather(at, ref["part_" + n], ref["w" + n], ref["gather_send"].at[i], ref["gather_recv"].at[i])
             for i, n in enumerate("aml")
@@ -402,10 +422,15 @@
         )
         early_parts, middle_parts, late_parts = ((0, 384, 0),), ((128, 640, 0), (0, 128, 4)), ((0, 512, 0),)
         first.along_z()
-        first.own_on()
-        second.own_on()
+        first.own_on(met=False)
+        second.along_z()
+        second.own_on(met=False)
+        third.along_z()
         for n in "aml":
             ref["w" + n][at.c, at.a, at.b, at.z] = ref["part_" + n][...]
+
+    else:
+        pl.semaphore_wait(barrier, len(peers))
 
     lane = iota((64, 128), 1)
     low_lanes = lane < 64
@@ -435,14 +460,23 @@
     for k in range(TILES):
         wt[k] = tile_weights(k, me, tensors, valid_len)
     if fast:
-        first.after_z(1, 3, 2)
-        second.along_z()
-        first.after_b(0, 1, 3, 2)
-        second.after_b(0)
+        first.after_z(1, 3, 2, met=False)
+        first.after_b(0, 1, 3, 2, met=False)
+        second.after_b(0, met=False)
+
+        @pl.when(at.c == 0)
+        def _():
+            pl.semaphore_wait(ref["ready"], len(others))
+
+        for j in range(4):
+            first.across(j, 0, 0)
+        for j in range(4):
+            first.across(j, 0, 1)
+        second.across(0, 0, 0)
+        second.across(0, 0, 1)
         first.after_a(0, 0, 1, 3, 2)
         first.after_a(1, 0, 1, 3, 2)
-        second.after_a(0, 0)
-        third.own_on()
+        second.after_z(1, 3, 2)
         first.after_across()
     for t in range(PAIRS):
         joint = nn(n1b[:, :256], get(wa, t, 0, 0, 384)) + nn(n1b[:, 256:], get(wa, t, 1, 0, 384))
@@ -533,8 +567,9 @@
 
     lax.fori_loop(0, PAIRS, pooling, 0)
     if fast:
-        second.after_z(1, 3)
-        third.along_z()
+        second.after_b(1, 3, 2)
+        third.own_on()
+        third.after_z(1, 3, 2)
 
     def attend(p, carry):
         exchanged(*halos(p))
@@ -559,27 +594,6 @@
             ns[here, :] = joined(nn(low, vw[p, keys, :]))
             ml[p, here, :] = joined(jnp.broadcast_to(m, (128, 128)))
             ds_[here, :] = joined(jnp.broadcast_to(total, (128, 128)))
-            if fast and k == 3:
-
-                @pl.when(p == 1)
-                def _():
-                    second.after_b(3)
-                    second.after_a(0, 1)
-
-                @pl.when(p == 2)
-                def _():
-                    second.after_a(1, 1)
-                    second.after_a(0, 2)
-                    third.after_z(1)
-                    third.after_a(0, 0)
-
-                @pl.when(p == 3)
-                def _():
-                    second.after_a(1, 2)
-                    third.after_z(2)
-                    third.after_b(1)
-                    third.after_a(1, 0)
-
         rows = slice(AT[5], AT[5] + 8)
         num, top, den = ns[rows, :], ml[p, rows, :], ds_[rows, :]
         for level in range(LEVELS - 2, -1, -1):
@@ -600,25 +614,19 @@
 
             @pl.when(p == 0)
             def _():
-                second.after_z(2)
-                second.after_b(1)
-                second.after_a(1, 0)
+                second.after_a(0, 0, 1, 3, 2)
 
             @pl.when(p == 1)
             def _():
-                second.after_b(2)
-                second.after_a(0, 3)
-                third.after_b(0)
+                third.after_b(0, 1, 3, 2)
 
             @pl.when(p == 2)
             def _():
-                second.after_a(1, 3)
-                third.after_z(3)
+                second.after_a(1, 0, 1, 3, 2)
 
             @pl.when(p == 3)
             def _():
-                third.after_a(0, 1)
-                third.after_b(3)
+                third.after_a(0, 0, 1, 3, 2)
 
         return carry
 
@@ -639,10 +647,6 @@
     n2s[...] = n2
     n2b = n2.astype(BF)
     n2t = n2b.T
-    if fast:
-        third.after_b(2)
-        third.after_a(0, 3)
-        third.after_a(1, 1)
     cotb = ref["cots"][...].astype(BF)
     cott = cotb.T
 
@@ -657,12 +661,8 @@
             put(gl, t, y, 0, 512, nn(cott[256 * y : 256 * y + 256, :], act))
         if fast:
             late.across(t, 0, 512, 0)
-            if t == 1:
-                third.after_a(0, 2)
-            if t == 2:
-                third.after_a(1, 3)
-    if fast:
-        third.after_a(1, 2)
+    if fast:
+        third.after_a(1, 0, 1, 3, 2)
         third.after_across()
         late.across_all(late_parts)
     dense, dn2 = [0.0, 0.0], [0.0, 0.0]
@@ -765,18 +765,15 @@
 
                 @pl.when(p == 1)
                 def _():
-                    late.own(outs["l"], 1)
-                    middle_sum.far(3)
+                    late.near(0)
 
                 @pl.when(p == 2)
                 def _():
-                    middle_sum.far(2)
-                    late.own(outs["l"], 2)
+                    late.own(outs["l"], 1)
 
                 @pl.when(p == 3)
                 def _():
-                    late.own(outs["l"], 0)
-                    middle_sum.far(0)
+                    middle_sum.near(1)
 
         for which in range(2):
             row = which * PAIRS + p
@@ -792,8 +789,7 @@
             @pl.when(p == 0)
             def _():
                 middle_sum.across_all(middle_parts)
-                middle_sum.far(1)
-                late.near(0)
+                middle_sum.far(1, 3, 2, 0)
 
             @pl.when(p == 1)
             def _():
@@ -801,10 +797,11 @@
 
             @pl.when(p == 2)
             def _():
-                middle_sum.near(1)
+                late.own(outs["l"], 2)
 
             @pl.when(p == 3)
             def _():
+                late.own(outs["l"], 0)
                 middle_sum.near(3)
 
         return carry
@@ -854,6 +851,7 @@
 
     lax.fori_loop(0, PAIRS, unpool, 0)
     if fast:
+        middle_sum.near(2, 0)
         middle_sum.own(outs["m"], 1)
 
     n1 = n1s[...]
@@ -884,22 +882,18 @@
             small_ref[...] = got[2 * i] + got[2 * i + 1]
 
         sum_send(0)
-        middle_sum.near(2)
         early.across_all(early_parts)
         early.far(1, 3, 2, 0)
         sum_add(0)
         sum_send(1)
-        middle_sum.own(outs["m"], 3)
-        middle_sum.near(0)
+        middle_sum.own(outs["m"], 3, 2, 0)
         sum_add(1)
         sum_send(2)
-        middle_sum.own(outs["m"], 2)
         early.near(1, 3, 2, 0)
         sum_add(2)
         got[6 + at.z] = small_ref[...]
         for k in range(1, 4):
             sums.send(2 + k, got.at[6 + at.z], got.at[6 + at.z], at.to_z(k))
-        middle_sum.own(outs["m"], 0)
         early.own(outs["a"], 1, 3, 2, 0)
     r1 = lax.rsqrt(row_variance(ref["xs"][...]) + EPS)
     in_grad = n2s[...] + norm_back(n1, r1, dn1)
@@ -1007,6 +1001,7 @@
             "gather_recv": pltpu.SemaphoreType.DMA((3, 31)),
             "reduce_send": pltpu.SemaphoreType.DMA((3, 23)),
             "reduce_recv": pltpu.SemaphoreType.DMA((3, 23)),
+            "ready": pltpu.SemaphoreType.REGULAR,
             "sum_send": pltpu.SemaphoreType.DMA((6,)),
             "sum_recv": pltpu.SemaphoreType.DMA((6,)),
         }

time: 97 us -> 95.1 us (0.980)
  Pallas kernels: 95.3 us -> 93.5 us
    pallas_call x1, Pallas kernels: 93.1 us -> 91.3 us  [run_layer(): pl.pallas_call(functools.partial(layer_kernel, fast, tensors, (*ins, *out...]
where the time goes in v5:
time: 95.1 us; the launch traced here: 94.9 us
  Pallas kernels  93.5 us (98%)
  between operations  1.46 us (2%)
    pallas_call x1, Pallas kernels, run_layer(): pl.pallas_call(functools.partial(layer_kernel, fast, tensors, (*ins, *out...  91.3 us
    pallas_call x1, Pallas kernels, hand_out(): pl.pallas_call(hand_out_kernel, out_shape=tuple((jax.ShapeDtypeStruct(sha...  2.18 us

profile of v5, /device:TPU:0, one launch (start us, length us, event | category | flops | bytes accessed | tf_op | source)
XLA Modules:
  0.0 94.9 jit_solution(14864590506642713096)
XLA Ops:
  1.3 91.3 %layer.1 = (bf16[256,1024]{1,0:T(8,128)(2,1)}, f32[64,1664]{1,0:T(8,128)}) custom-call(s32[1]{0:T(128)S(6)} %copy.22.refs_0_, bf16[256,512]{1,0:T(8,128)(2,1)} %refs_1_.1, bf16[256,512]{1,0:T(8,128)(2,1)} %refs_2_.1, bf16[64,128]{1,0:T(8,128)(2,1)} %refs_3_.1, bf16[64,128]{1,0:T(8,128)(2,1)} %refs_4_.1, bf16[64,128]{1,0:T(8,128)(2,1)} %refs_5_.1, ...), custom_call_target="tpu_custom_call" | custom-call | tf_op jit(solution)/shard_map/layer/pallas_call | solution.py:1012
  92.6 2.2 %hand_out.1 = (bf16[256,512]{1,0:T(8,128)(2,1)}, bf16[256,512]{1,0:T(8,128)(2,1)}, f32[64,128]{1,0:T(8,128)}, f32[64,128]{1,0:T(8,128)}, f32[64,128]{1,0:T(8,128...) custom-call(bf16[256,1024]{1,0:T(8,128)(2,1)} %get-tuple-element.24., ...), custom_call_target="tpu_custom_call" | custom-call | tf_op jit(solution)/shard_map/hand_out/pallas_call | solution.py:1043

commit v6 on v5

--- a/solution.py
+++ b/solution.py
@@ -773,7 +773,7 @@
 
                 @pl.when(p == 3)
                 def _():
-                    middle_sum.near(1)
+                    late.own(outs["l"], 0)
 
         for which in range(2):
             row = which * PAIRS + p
@@ -801,8 +801,7 @@
 
             @pl.when(p == 3)
             def _():
-                late.own(outs["l"], 0)
-                middle_sum.near(3)
+                middle_sum.near(1)
 
         return carry
 
@@ -851,8 +850,7 @@
 
     lax.fori_loop(0, PAIRS, unpool, 0)
     if fast:
-        middle_sum.near(2, 0)
-        middle_sum.own(outs["m"], 1)
+        middle_sum.near(3, 2)
 
     n1 = n1s[...]
     n1t = n1.astype(BF).T
@@ -881,6 +879,8 @@
             sums.arrived(i, got.at[2 * i + 1], ways[i])
             small_ref[...] = got[2 * i] + got[2 * i + 1]
 
+        middle_sum.near(0)
+        middle_sum.own(outs["m"], 1)
         sum_send(0)
         early.across_all(early_parts)
         early.far(1, 3, 2, 0)

time: 95.1 us -> 94.2 us (level)
  Pallas kernels: 93.5 us -> 92.5 us
where the time goes in v6:
time: 94.2 us; the launch traced here: 94 us
  Pallas kernels  92.5 us (98%)
  between operations  1.46 us (2%)
    pallas_call x1, Pallas kernels, run_layer(): pl.pallas_call(functools.partial(layer_kernel, fast, tensors, (*ins, *out...  90.4 us
    pallas_call x1, Pallas kernels, hand_out(): pl.pallas_call(hand_out_kernel, out_shape=tuple((jax.ShapeDtypeStruct(sha...  2.18 us

profile of v6, /device:TPU:0, one launch (start us, length us, event | category | flops | bytes accessed | tf_op | source)
XLA Modules:
  0.0 94.0 jit_solution(1018243716341182069)
XLA Ops:
  1.3 90.4 %layer.1 = (bf16[256,1024]{1,0:T(8,128)(2,1)}, f32[64,1664]{1,0:T(8,128)}) custom-call(s32[1]{0:T(128)S(6)} %copy.22.refs_0_, bf16[256,512]{1,0:T(8,128)(2,1)} %refs_1_.1, bf16[256,512]{1,0:T(8,128)(2,1)} %refs_2_.1, bf16[64,128]{1,0:T(8,128)(2,1)} %refs_3_.1, bf16[64,128]{1,0:T(8,128)(2,1)} %refs_4_.1, bf16[64,128]{1,0:T(8,128)(2,1)} %refs_5_.1, ...), custom_call_target="tpu_custom_call" | custom-call | tf_op jit(solution)/shard_map/layer/pallas_call | solution.py:1012
  91.7 2.2 %hand_out.1 = (bf16[256,512]{1,0:T(8,128)(2,1)}, bf16[256,512]{1,0:T(8,128)(2,1)}, f32[64,128]{1,0:T(8,128)}, f32[64,128]{1,0:T(8,128)}, f32[64,128]{1,0:T(8,128...) custom-call(bf16[256,1024]{1,0:T(8,128)(2,1)} %get-tuple-element.24., ...), custom_call_target="tpu_custom_call" | custom-call | tf_op jit(solution)/shard_map/hand_out/pallas_call | solution.py:1043
